TPU v7x, 512 devices: a whole 4x8x8 slice. The times are simulated.
512 devices in a mesh: leaf: 32 (over y, x), node: 16 (over z, core).
Axes of the slice: x: 4, y: 8, z: 8, core: 2. Of those that a mesh axis runs over, the one named last changes fastest.
Arguments:
- positions: float32 [3, 524288], P(None, ('leaf', 'node')), may hold values from 0 to 64, as said below
- charges: float32 [524288], P(('leaf', 'node')), may hold values from -0.625 to 0.625
- near_list: int32 [1024, 26], P(('leaf', 'node')), may hold values from 0 to 1023, as said below
- near_count: int32 [1024], P(('leaf', 'node')), may hold values from 1 to 26, as said below
- far_sample: float32 [524288, 128], P(('leaf', 'node')), may hold values from -0.625 to 0.625
- proxies: float32 [1024, 3, 128], P(('leaf', 'node')), may hold values from -2 to 66, as said below
- strengths: float32 [1024, 128], P(('leaf', 'node')), may hold values from 0.005 to 0.05
Outputs:
- near_potential: float32 [524288], P(('leaf', 'node'))
- leaf_coeffs: float32 [1024, 128], P(('leaf', 'node'))
- top_factor: float32 [32, 128, 128], P('leaf', 'node')
- top_coeffs: float32 [32, 128], P('leaf', 'node')
Inputs may be any that keep to these rules, and one draw needn't show every extreme that they name: `near_list`: each entry of row g is a leaf other than g whose cube touches the cube of leaf g (shares a face, an edge or a corner); the entries before near_count[g] are distinct. `near_count`: slots of a row at or past its count are not used; some leaf uses all 26 slots. `positions`: the particles of leaf g lie in the unit cube whose lowest corner is (g // 16, (g // 4) % 4, g % 4). `proxies`: the proxy points of leaf g lie at distance 1.5 to 2 from the centre of its cube.
All inputs are finite; a program needn't handle non-finite values.
Results may differ from a plain program's by a relative error of at most 0.0003.
Values sent between devices are 32-bit elements; how exact they have to be, the bound alone decides.
A program may use at most 64 MiB of HBM per device.

v0:
```python
import jax
import jax.numpy as jnp
from jax import lax
from jax.sharding import PartitionSpec as P

soft_square = 0.0025


def from_partner(block, axis, apart):
    count = lax.axis_size(axis)
    route = []
    for low in range(count):
        high = low | 1 << apart
        if high != low and high < count:
            route += [(low, high), (high, low)]
    return lax.ppermute(block, axis, route)


def extended(block, sides, width):
    for axis, dim in sides:
        count = lax.axis_size(axis)
        forward = [(i, i + 1) for i in range(count - 1)]
        backward = [(target, source) for source, target in forward]
        low = lax.ppermute(
            lax.slice_in_dim(block, block.shape[dim] - width, None, axis=dim), axis, forward
        )
        high = lax.ppermute(lax.slice_in_dim(block, 0, width, axis=dim), axis, backward)
        block = jnp.concatenate([low, block, high], axis=dim)
    return block


def leaf_basis(points, weights, sample, proxies, strengths):
    highest = lax.Precision.HIGHEST
    square_sum = jnp.zeros(sample.shape, jnp.float32)
    for component in range(3):
        separation = points[:, component, :, None] - proxies[:, component, None, :]
        square_sum = square_sum + separation * separation
    response = sample + lax.rsqrt(square_sum + soft_square) * strengths[:, None, :]
    gram_matrix = jnp.einsum("npr,nps->nrs", response, response, precision=highest)
    moment = jnp.einsum("npr,np->nr", response, weights, precision=highest)
    factor = jnp.linalg.cholesky(gram_matrix)
    coeffs = lax.linalg.triangular_solve(factor, moment[..., None], left_side=True, lower=True)[
        ..., 0
    ]
    return (factor, coeffs)


def merge_pair(left_factor, left_coeffs, right_factor, right_coeffs):
    highest = lax.Precision.HIGHEST
    gram_matrix = jnp.matmul(left_factor, jnp.swapaxes(left_factor, -1, -2), precision=highest)
    gram_matrix = gram_matrix + jnp.matmul(
        right_factor, jnp.swapaxes(right_factor, -1, -2), precision=highest
    )
    factor = jnp.linalg.cholesky(gram_matrix)
    moment = jnp.matmul(left_factor, left_coeffs[..., None], precision=highest)
    moment = moment + jnp.matmul(right_factor, right_coeffs[..., None], precision=highest)
    coeffs = lax.linalg.triangular_solve(factor, moment, left_side=True, lower=True)[..., 0]
    return (factor, coeffs)


def tile_sum(target, source):
    square_sum = jnp.zeros((target.shape[1], source.shape[1]), jnp.float32)
    for component in range(3):
        separation = target[component][:, None] - source[component][None, :]
        square_sum = square_sum + separation * separation
    return jnp.dot(lax.rsqrt(square_sum + soft_square), source[3], precision=lax.Precision.HIGHEST)


def body(positions, charges, near_list, near_count, far_sample, proxies, strengths):
    per_device = near_count.shape[0]
    leaf_size = charges.shape[0] // per_device
    rank_width = far_sample.shape[1]
    node_count = lax.axis_size("node")
    node_index = lax.axis_index("node")
    block_index = lax.axis_index("leaf")
    group_size = per_device * node_count
    points = positions.reshape(3, per_device, leaf_size).transpose(1, 0, 2)
    weights = charges.reshape(per_device, leaf_size)
    factor, coeffs = leaf_basis(
        points, weights, far_sample.reshape(per_device, leaf_size, rank_width), proxies, strengths
    )
    leaf_coeffs = coeffs
    while factor.shape[0] > 1:
        factor, coeffs = merge_pair(factor[0::2], coeffs[0::2], factor[1::2], coeffs[1::2])
    for level in range(node_count.bit_length() - 1):
        other_factor, other_coeffs = from_partner((factor, coeffs), "node", level)
        upper = node_index >> level & 1 == 1
        left_factor = jnp.where(upper, other_factor, factor)
        right_factor = jnp.where(upper, factor, other_factor)
        left_coeffs = jnp.where(upper, other_coeffs, coeffs)
        right_coeffs = jnp.where(upper, coeffs, other_coeffs)
        factor, coeffs = merge_pair(left_factor, left_coeffs, right_factor, right_coeffs)
    row_share = rank_width // node_count
    row_start = node_index * row_share
    factor = lax.dynamic_slice_in_dim(factor, row_start, row_share, 1)
    coeffs = lax.dynamic_slice_in_dim(coeffs, row_start, row_share, 1)
    packed = jnp.concatenate([positions, charges[None, :]], 0)
    group_points = lax.all_gather(packed, "node", axis=1, tiled=True)
    window = extended(group_points, (("leaf", 1),), group_size * leaf_size)
    window_start = block_index * group_size - group_size

    def source_at(index):
        start = (index - window_start) * leaf_size
        return lax.dynamic_slice_in_dim(window, start, leaf_size, 1)

    self_terms = []
    for member in range(per_device):
        own_points = packed[:, member * leaf_size : (member + 1) * leaf_size]
        self_terms.append(tile_sum(own_points, own_points))
    pieces = []
    for member in range(per_device):
        own_points = packed[:, member * leaf_size : (member + 1) * leaf_size]
        near_row = near_list[member]

        def add_pair(slot, running, own_points=own_points, near_row=near_row):
            return running + tile_sum(own_points, source_at(near_row[slot]))

        near_total = lax.fori_loop(
            0, near_count[member], add_pair, jnp.zeros((leaf_size,), jnp.float32)
        )
        pieces.append(self_terms[member] + near_total)
    near_potential = jnp.concatenate(pieces)
    return (near_potential, leaf_coeffs, factor, coeffs)


def solution(mesh):
    in_specs = (
        P(None, ("leaf", "node")),
        P(("leaf", "node")),
        P(("leaf", "node"), None),
        P(("leaf", "node")),
        P(("leaf", "node"), None),
        P(("leaf", "node"), None, None),
        P(("leaf", "node"), None),
    )
    out_specs = (
        P(("leaf", "node")),
        P(("leaf", "node"), None),
        P("leaf", "node", None),
        P("leaf", "node"),
    )
    return jax.shard_map(body, mesh=mesh, in_specs=in_specs, out_specs=out_specs, check_vma=False)
```

profile of v0, /device:TPU:160, one launch (start us, length us, event | category | flops | bytes accessed | tf_op | source)
XLA Modules:
  0.0 380.6 jit_solution(11427658547299788725)
XLA Ops:
  1.4 19.9 %all_gather.3 = f32[4,16384]{1,0:T(4,128)S(1)} all-gather(f32[4,1024]{1,0:T(4,128)S(1)} %pad_maximum_fusion), channel_id=1, replica_groups=mesh['leaf'=32,'node'=16] {'node'}, dimensions={1}, use_global_device_ids=true | all-gather | bytes 278528 | tf_op jit(solution)/shard_map/all_gather | solution.py:98
  21.3 3.4 collective-permute-start
  24.7 5.8 %collective-permute-start.1 = (f32[4,16384]{1,0:T(4,128)S(1)}, f32[4,16384]{1,0:T(4,128)S(1)}, u32[]{:S(2)}, u32[]{:S(2)}) collective-permute-start(f32[4,16384]{1,0:T(4,128)S(1)} %all_gather.3), channel_id=1, source_target_pairs={{16,0},{32,16},{48,32},{64,48},{80,64},{96,80},{112,96},{128,112},... | collective-permute-start | bytes 786440 | tf_op jit(solution)/shard_map/ppermute | solution.py:27
  34.6 23.5 %custom-call.13 = f32[2,128,128]{2,1,0:T(8,128)S(1)} custom-call(f32[2,128,128]{2,1,0:T(8,128)S(1)} %fusion.87), custom_call_target="Cholesky" | custom-call | tf_op jit(solution)/shard_map/jit(cholesky)/cholesky | solution.py:41
  58.3 20.2 %custom-call.14 = f32[2,1,128,128]{2,3,1,0:T(8,128)S(1)} custom-call(f32[2,1,128,128]{3,2,1,0:T(8,128)S(1)} %get-tuple-element.122), custom_call_target="InvertDiagBlocksLowerTriangular" | custom-call | tf_op jit(solution)/shard_map/triangular_solve | solution.py:42
  81.1 11.7 %custom-call.23 = f32[1,128,128]{2,1,0:T(8,128)S(1)} custom-call(f32[1,128,128]{2,1,0:T(8,128)S(1)} %fusion.104), custom_call_target="Cholesky" | custom-call | tf_op jit(solution)/shard_map/jit(cholesky)/cholesky | solution.py:54
  94.1 9.8 %custom-call.28 = f32[1,1,128,128]{2,3,1,0:T(8,128)S(1)} custom-call(f32[1,1,128,128]{3,2,1,0:T(8,128)S(1)} %get-tuple-element.120), custom_call_target="InvertDiagBlocksLowerTriangular" | custom-call | tf_op jit(solution)/shard_map/triangular_solve/custom-call.3 | solution.py:57
  104.1 1.9 collective-permute-start.6
  106.0 2.6 collective-permute-start.2
  110.7 1.4 fusion.48
  113.4 11.7 %custom-call.24 = f32[1,128,128]{2,1,0:T(8,128)S(1)} custom-call(f32[1,128,128]{2,1,0:T(8,128)S(1)} %fusion.100), custom_call_target="Cholesky" | custom-call | tf_op jit(solution)/shard_map/jit(cholesky)/cholesky | solution.py:54
  126.4 9.8 %custom-call.29 = f32[1,1,128,128]{2,3,1,0:T(8,128)S(1)} custom-call(f32[1,1,128,128]{3,2,1,0:T(8,128)S(1)} %get-tuple-element.118), custom_call_target="InvertDiagBlocksLowerTriangular" | custom-call | tf_op jit(solution)/shard_map/triangular_solve/custom-call.3 | solution.py:57
  136.2 1.9 collective-permute-start.3
  138.8 4.1 %collective-permute-start.7 = (f32[1,128]{1,0:T(1,128)S(1)}, f32[1,128]{1,0:T(1,128)S(1)}, u32[]{:S(2)}, u32[]{:S(2)}) collective-permute-start(f32[1,128]{1,0:T(1,128)S(1)} %fusion.110), channel_id=1, source_target_pairs={{0,2},{2,0},{1,3},{3,1},{4,6},{6,4},{5,7},{7,5},{8,10},{10,8},{9,1... | collective-permute-start | bytes 1544 | tf_op jit(solution)/shard_map/ppermute | solution.py:16
  143.6 11.7 %custom-call.25 = f32[1,128,128]{2,1,0:T(8,128)S(1)} custom-call(f32[1,128,128]{2,1,0:T(8,128)S(1)} %fusion.96), custom_call_target="Cholesky" | custom-call | tf_op jit(solution)/shard_map/jit(cholesky)/cholesky | solution.py:54
  156.7 9.8 %custom-call.30 = f32[1,1,128,128]{2,3,1,0:T(8,128)S(1)} custom-call(f32[1,1,128,128]{3,2,1,0:T(8,128)S(1)} %get-tuple-element.116), custom_call_target="InvertDiagBlocksLowerTriangular" | custom-call | tf_op jit(solution)/shard_map/triangular_solve/custom-call.3 | solution.py:57
  166.5 4.6 %collective-permute-start.4 = (f32[1,128,128]{2,1,0:T(8,128)S(1)}, f32[1,128,128]{2,1,0:T(8,128)S(1)}, u32[]{:S(2)}, u32[]{:S(2)}) collective-permute-start(f32[1,128,128]{2,1,0:T(8,128)S(1)} %get-tuple-element.117), channel_id=1, source_target_pairs={{0,4},{4,0},{1,5},{5,1},{2,6},{6,2},{3,7},{7,3},{8,12},{12,8},{9,1... | collective-permute-start | bytes 196616 | tf_op jit(solution)/shard_map/ppermute | solution.py:16
  171.7 2.4 collective-permute-start.8
  174.8 11.7 %custom-call.26 = f32[1,128,128]{2,1,0:T(8,128)S(1)} custom-call(f32[1,128,128]{2,1,0:T(8,128)S(1)} %fusion.92), custom_call_target="Cholesky" | custom-call | tf_op jit(solution)/shard_map/jit(cholesky)/cholesky | solution.py:54
  187.8 9.8 %custom-call.31 = f32[1,1,128,128]{2,3,1,0:T(8,128)S(1)} custom-call(f32[1,1,128,128]{3,2,1,0:T(8,128)S(1)} %get-tuple-element.114), custom_call_target="InvertDiagBlocksLowerTriangular" | custom-call | tf_op jit(solution)/shard_map/triangular_solve/custom-call.3 | solution.py:57
  197.6 4.3 %collective-permute-start.5 = (f32[1,128,128]{2,1,0:T(8,128)S(1)}, f32[1,128,128]{2,1,0:T(8,128)S(1)}, u32[]{:S(2)}, u32[]{:S(2)}) collective-permute-start(f32[1,128,128]{2,1,0:T(8,128)S(1)} %get-tuple-element.115), channel_id=1, source_target_pairs={{0,8},{8,0},{1,9},{9,1},{2,10},{10,2},{3,11},{11,3},{4,12},{12,4},... | collective-permute-start | bytes 196616 | tf_op jit(solution)/shard_map/ppermute | solution.py:16
  202.5 5.8 %collective-permute-start.9 = (f32[1,128]{1,0:T(1,128)S(1)}, f32[1,128]{1,0:T(1,128)S(1)}, u32[]{:S(2)}, u32[]{:S(2)}) collective-permute-start(f32[1,128]{1,0:T(1,128)S(1)} %fusion.114), channel_id=1, source_target_pairs={{0,8},{8,0},{1,9},{9,1},{2,10},{10,2},{3,11},{11,3},{4,12},{12,4},... | collective-permute-start | bytes 1544 | tf_op jit(solution)/shard_map/ppermute | solution.py:16
  209.1 11.7 %custom-call.27 = f32[1,128,128]{2,1,0:T(8,128)S(1)} custom-call(f32[1,128,128]{2,1,0:T(8,128)S(1)} %fusion.88), custom_call_target="Cholesky" | custom-call | tf_op jit(solution)/shard_map/jit(cholesky)/cholesky | solution.py:54
  222.2 9.8 %custom-call.32 = f32[1,1,128,128]{2,3,1,0:T(8,128)S(1)} custom-call(f32[1,1,128,128]{3,2,1,0:T(8,128)S(1)} %get-tuple-element.112), custom_call_target="InvertDiagBlocksLowerTriangular" | custom-call | tf_op jit(solution)/shard_map/triangular_solve/custom-call.3 | solution.py:57
  233.9 58.3 %while.20 = (s32[]{:T(128)}, f32[512]{0:T(512)S(1)}, s32[]{:T(128)}, f32[4,512]{1,0:T(4,128)S(1)}, s32[26]{0:T(128)S(1)}, /*index=5*/s32[]{:T(128)}, f32[4,49152...) while((s32[]{:T(128)}, f32[512]{0:T(512)S(1)}, ...), condition=%wide.region_1.2_spmd, body=%wide.region_0.1_spmd.sunk | while | flops 5505549 | bytes 47405 | solution.py:118
  239.2 1.4 fusion.199
  246.0 1.4 fusion.199
  249.4 1.4 fusion.199
  256.2 1.4 fusion.199
  259.6 1.4 fusion.199
  266.4 1.4 fusion.199
  269.8 1.4 fusion.199
  276.5 1.4 fusion.199
  283.3 1.4 fusion.199
  286.7 1.4 fusion.199
  292.2 87.3 %while.21 = (s32[]{:T(128)}, f32[512]{0:T(512)S(1)}, s32[]{:T(128)}, f32[4,512]{1,0:T(4,128)S(1)}, s32[26]{0:T(128)S(1)}, /*index=5*/s32[]{:T(128)}, f32[4,49152...) while((s32[]{:T(128)}, f32[512]{0:T(512)S(1)}, ...), condition=%wide.region_3.4_spmd, body=%wide.region_2.3_spmd.sunk | while | flops 5505549 | bytes 47405 | solution.py:118
  294.1 1.4 fusion.201
  304.1 1.4 fusion.201
  307.4 1.4 fusion.201
  310.8 1.4 fusion.201
  320.8 1.4 fusion.201
  324.1 1.4 fusion.201
  327.5 1.4 fusion.201
  334.1 1.4 fusion.201
  337.5 1.4 fusion.201
  340.8 1.4 fusion.201
  350.8 1.4 fusion.201
  354.1 1.4 fusion.201
  (254 shorter events, 83.7 us)
Async XLA Ops:
  1.4 29.1 %copy-start = (f32[3,1024]{1,0:T(4,128)S(1)}, f32[3,1024]{1,0:T(4,128)}, u32[]{:S(2)}) copy-start(f32[3,1024]{1,0:T(4,128)} %param.14) | copy-start | bytes 36868
  21.3 200.1 %collective-permute-start = (f32[4,16384]{1,0:T(4,128)S(1)}, f32[4,16384]{1,0:T(4,128)S(1)}, u32[]{:S(2)}, u32[]{:S(2)}) collective-permute-start(f32[4,16384]{1,0:T(4,128)S(1)} %all_gather.3), channel_id=1, source_target_pairs={{0,16},{16,32},{32,48},{48,64},{64,80},{80,96},{96,112},{112,128},... | collective-permute-start | bytes 786440 | tf_op jit(solution)/shard_map/ppermute | solution.py:24
  24.7 209.1 %collective-permute-start.1 = (f32[4,16384]{1,0:T(4,128)S(1)}, f32[4,16384]{1,0:T(4,128)S(1)}, u32[]{:S(2)}, u32[]{:S(2)}) collective-permute-start(f32[4,16384]{1,0:T(4,128)S(1)} %all_gather.3), channel_id=1, source_target_pairs={{16,0},{32,16},{48,32},{64,48},{80,64},{96,80},{112,96},{128,112},... | collective-permute-start | bytes 786440 | tf_op jit(solution)/shard_map/ppermute | solution.py:27
  30.6 0.7 copy-start.3
  32.5 0.7 copy-start.6
  58.3 20.2 %copy-start.1 = (f32[1024]{0:T(1024)S(1)}, f32[1024]{0:T(1024)}, u32[]{:S(2)}) copy-start(f32[1024]{0:T(1024)} %param.15) | copy-start | bytes 12292
  79.9 0.6 copy-start.2
  104.1 34.1 %collective-permute-start.6 = (f32[1,128]{1,0:T(1,128)S(1)}, f32[1,128]{1,0:T(1,128)S(1)}, u32[]{:S(2)}, u32[]{:S(2)}) collective-permute-start(f32[1,128]{1,0:T(1,128)S(1)} %fusion.108), channel_id=1, source_target_pairs={{0,1},{1,0},{2,3},{3,2},{4,5},{5,4},{6,7},{7,6},{8,9},{9,8},{10,11... | collective-permute-start | bytes 1544 | tf_op jit(solution)/shard_map/ppermute | solution.py:16
  106.0 6.7 %collective-permute-start.2 = (f32[1,128,128]{2,1,0:T(8,128)S(1)}, f32[1,128,128]{2,1,0:T(8,128)S(1)}, u32[]{:S(2)}, u32[]{:S(2)}) collective-permute-start(f32[1,128,128]{2,1,0:T(8,128)S(1)} %get-tuple-element.121), channel_id=1, source_target_pairs={{0,1},{1,0},{2,3},{3,2},{4,5},{5,4},{6,7},{7,6},{8,9},{9,8},{10,11... | collective-permute-start | bytes 196616 | tf_op jit(solution)/shard_map/ppermute | solution.py:16
  108.7 0.7 copy-start.5
  110.7 1.4 copy-start.4
  136.2 6.7 %collective-permute-start.3 = (f32[1,128,128]{2,1,0:T(8,128)S(1)}, f32[1,128,128]{2,1,0:T(8,128)S(1)}, u32[]{:S(2)}, u32[]{:S(2)}) collective-permute-start(f32[1,128,128]{2,1,0:T(8,128)S(1)} %get-tuple-element.119), channel_id=1, source_target_pairs={{0,2},{2,0},{1,3},{3,1},{4,6},{6,4},{5,7},{7,5},{8,10},{10,8},{9,1... | collective-permute-start | bytes 196616 | tf_op jit(solution)/shard_map/ppermute | solution.py:16
  138.8 32.3 %collective-permute-start.7 = (f32[1,128]{1,0:T(1,128)S(1)}, f32[1,128]{1,0:T(1,128)S(1)}, u32[]{:S(2)}, u32[]{:S(2)}) collective-permute-start(f32[1,128]{1,0:T(1,128)S(1)} %fusion.110), channel_id=1, source_target_pairs={{0,2},{2,0},{1,3},{3,1},{4,6},{6,4},{5,7},{7,5},{8,10},{10,8},{9,1... | collective-permute-start | bytes 1544 | tf_op jit(solution)/shard_map/ppermute | solution.py:16
  166.5 7.6 %collective-permute-start.4 = (f32[1,128,128]{2,1,0:T(8,128)S(1)}, f32[1,128,128]{2,1,0:T(8,128)S(1)}, u32[]{:S(2)}, u32[]{:S(2)}) collective-permute-start(f32[1,128,128]{2,1,0:T(8,128)S(1)} %get-tuple-element.117), channel_id=1, source_target_pairs={{0,4},{4,0},{1,5},{5,1},{2,6},{6,2},{3,7},{7,3},{8,12},{12,8},{9,1... | collective-permute-start | bytes 196616 | tf_op jit(solution)/shard_map/ppermute | solution.py:16
  171.7 30.2 %collective-permute-start.8 = (f32[1,128]{1,0:T(1,128)S(1)}, f32[1,128]{1,0:T(1,128)S(1)}, u32[]{:S(2)}, u32[]{:S(2)}) collective-permute-start(f32[1,128]{1,0:T(1,128)S(1)} %fusion.112), channel_id=1, source_target_pairs={{0,4},{4,0},{1,5},{5,1},{2,6},{6,2},{3,7},{7,3},{8,12},{12,8},{9,1... | collective-permute-start | bytes 1544 | tf_op jit(solution)/shard_map/ppermute | solution.py:16
  197.6 10.8 %collective-permute-start.5 = (f32[1,128,128]{2,1,0:T(8,128)S(1)}, f32[1,128,128]{2,1,0:T(8,128)S(1)}, u32[]{:S(2)}, u32[]{:S(2)}) collective-permute-start(f32[1,128,128]{2,1,0:T(8,128)S(1)} %get-tuple-element.115), channel_id=1, source_target_pairs={{0,8},{8,0},{1,9},{9,1},{2,10},{10,2},{3,11},{11,3},{4,12},{12,4},... | collective-permute-start | bytes 196616 | tf_op jit(solution)/shard_map/ppermute | solution.py:16
  202.5 29.5 %collective-permute-start.9 = (f32[1,128]{1,0:T(1,128)S(1)}, f32[1,128]{1,0:T(1,128)S(1)}, u32[]{:S(2)}, u32[]{:S(2)}) collective-permute-start(f32[1,128]{1,0:T(1,128)S(1)} %fusion.114), channel_id=1, source_target_pairs={{0,8},{8,0},{1,9},{9,1},{2,10},{10,2},{3,11},{11,3},{4,12},{12,4},... | collective-permute-start | bytes 1544 | tf_op jit(solution)/shard_map/ppermute | solution.py:16
where the time goes:
time: 388 us; the launch traced here: 381 us
  other arithmetic  160 us (41%)
  matrix products  70.1 us (18%)
  loops' own time  55.5 us (14%)
  starting transfers between devices  36.8 us (9%)
  local copies, waits for them, and re-layouts  36.3 us (9%)
  blocking collectives  19.9 us (5%)
    dot_general x45, matrix products, tile_sum(): jnp.dot(lax.rsqrt(square_sum + soft_square), source[3], precision=lax.Pre...  62.1 us
    another operation x15, other arithmetic, merge_pair(): factor = jnp.linalg.cholesky(gram_matrix)  61.9 us
    another operation x2, loops' own time, body(): lax.fori_loop(0, near_count[member], add_pair, jnp.zeros((leaf_size,), jn...  55.5 us
    another operation x10, other arithmetic, merge_pair(): lax.linalg.triangular_solve(factor, moment, left_side=True, lower=True)  52.3 us
    ppermute x8, starting transfers between devices, from_partner(): return lax.ppermute(block, axis, route)  27.6 us
    dynamic_slice x43, local copies, waits for them, and re-layouts, add_pair(): return running + tile_sum(own_points, source_at(near_row[slot]))  26.4 us
    another operation x4, other arithmetic, leaf_basis(): factor = jnp.linalg.cholesky(gram_matrix)  23.6 us
    another operation x3, other arithmetic, leaf_basis(): lax.linalg.triangular_solve(factor, moment[..., None], left_side=True, lo...  20.3 us
  transfers between devices with their start and end apart: 10, of which 1 were waited for; matrix products, arithmetic and copies ran while one was open for 45% of the time, Pallas kernels for 0%

commit v1 on v0

v1 whole, which is shorter than its diff:
```python
import functools

import jax
import jax.numpy as jnp
from jax import lax
from jax.experimental import pallas as pl
from jax.experimental.pallas import tpu as pltpu
from jax.sharding import PartitionSpec as P

soft_square = 0.0025
ACROSS = 4
PANEL = 16
CHUNK = 128
MESH = pl.DeviceIdType.MESH
HIGHEST = lax.Precision.HIGHEST


def split3(v):
    high = v.astype(jnp.bfloat16).astype(jnp.float32)
    rest = v - high
    mid = rest.astype(jnp.bfloat16).astype(jnp.float32)
    return high, mid, rest - mid


def feature_rows(xyz, fourth, fifth):
    row = lax.broadcasted_iota(jnp.int32, (8, xyz.shape[1]), 0)
    rows = jnp.where(row == 4, fifth, 0.0)
    rows = jnp.where(row == 3, fourth, rows)
    for k in range(3):
        rows = jnp.where(row == k, xyz[k : k + 1], rows)
    return split3(rows)


def source_features(xyz):
    high, mid, low = feature_rows(xyz, jnp.sum(xyz * xyz, 0, keepdims=True), 1.0)
    return jnp.concatenate([high, high, high, mid, mid, mid, low, low], 0).astype(jnp.bfloat16)


def target_features(xyz):
    norm = jnp.sum(xyz * xyz, 0, keepdims=True) + soft_square
    high, mid, low = feature_rows(-2.0 * xyz, 1.0, norm)
    return jnp.concatenate([high, mid, low, high, mid, low, high, mid], 0).T.astype(jnp.bfloat16)


def place(node):
    return node // 8, lax.rem(node // 2, ACROSS), lax.rem(node, 2)


def centre_of(block, node):
    slab, y, half = place(node)
    return (
        (2 * block + slab).astype(jnp.float32) + 0.5,
        y.astype(jnp.float32) + 0.5,
        (2 * half).astype(jnp.float32) + 1.0,
    )


def centred(rows, centre):
    row = lax.broadcasted_iota(jnp.int32, rows.shape, 0)
    shift = jnp.where(row == 0, centre[0], jnp.where(row == 1, centre[1], centre[2]))
    return rows - shift


def exchange_kernel(
    blocks,
    nodes,
    pos_ref,
    charge_ref,
    far_ref,
    proxy_ref,
    strength_ref,
    win_ref,
    gram_ref,
    moment_ref,
    top_gram_ref,
    top_moment_ref,
    share,
    parts,
    win_send,
    win_recv,
    rs_send,
    rs_recv,
    ag_send,
    ag_recv,
):
    block = lax.axis_index("leaf")
    node = lax.axis_index("node")
    slab, y, half = place(node)
    size = pos_ref.shape[1] // 2
    rank = far_ref.shape[1]

    def spatial(ds, dy, core):
        level = slab + ds
        step = (level + 2) // 2 - 1
        level = level - 2 * step
        other = level * 8 + lax.rem(y + dy + ACROSS, ACROSS) * 2 + core
        return (lax.rem(block + step + blocks, blocks), other)

    def in_block(k):
        return (block, lax.rem(node + k, nodes))

    outside = 1 - 2 * slab
    barrier = pltpu.get_barrier_semaphore()
    for k in range(1, nodes):
        pl.semaphore_signal(barrier, inc=1, device_id=in_block(k), device_id_type=MESH)
    for dy in (-1, 0, 1):
        for core in (0, 1):
            target = spatial(-outside, dy, core)
            pl.semaphore_signal(barrier, inc=1, device_id=target, device_id_type=MESH)

    for t in range(2):
        lanes = slice(t * size, (t + 1) * size)
        win_ref[4, t, 0:3, :] = pos_ref[:, lanes]
        win_ref[4, t, 3:4, :] = charge_ref[:, lanes]
    centre = centre_of(block, node)
    for t in range(2):
        lanes = slice(t * size, (t + 1) * size)
        distance = jnp.dot(
            target_features(centred(pos_ref[:, lanes], centre)),
            source_features(centred(proxy_ref[t], centre)),
            preferred_element_type=jnp.float32,
        )
        response = far_ref[lanes, :] + lax.rsqrt(distance) * strength_ref[t : t + 1, :]
        gram = lax.dot_general(
            response,
            response,
            (((0,), (0,)), ((), ())),
            precision=HIGHEST,
            preferred_element_type=jnp.float32,
        )
        moment = jnp.dot(
            jnp.broadcast_to(charge_ref[:, lanes], (8, size)),
            response,
            precision=HIGHEST,
            preferred_element_type=jnp.float32,
        )
        gram_ref[t] = gram
        moment_ref[t] = moment
    total = gram_ref[0] + gram_ref[1]
    total_moment = moment_ref[0, 0:1, :] + moment_ref[1, 0:1, :]
    rows = rank // nodes
    for n in range(nodes):
        share[n, 0:rows, :] = total[n * rows : (n + 1) * rows]
        share[n, rows : rows + 1, :] = total_moment

    pl.semaphore_wait(barrier, nodes - 1 + 6)

    rs = []
    for k in range(1, nodes):
        target = in_block(k)
        rs.append(
            pltpu.make_async_remote_copy(
                src_ref=share.at[target[1]],
                dst_ref=parts.at[node],
                send_sem=rs_send.at[k],
                recv_sem=rs_recv.at[k],
                device_id=target,
                device_id_type=MESH,
            )
        )
        rs[-1].start()
    window = []
    for ds in (-1, 0, 1):
        for dy in (-1, 0, 1):
            slot = 4 + 3 * ds + dy
            if slot != 4:
                window.append(
                    pltpu.make_async_remote_copy(
                        src_ref=win_ref.at[4, pl.ds(0, 2)],
                        dst_ref=win_ref.at[8 - slot, pl.ds(0, 2)],
                        send_sem=win_send.at[slot],
                        recv_sem=win_recv.at[slot],
                        device_id=spatial(ds, dy, half),
                        device_id_type=MESH,
                    )
                )
                window[-1].start()
            window.append(
                pltpu.make_async_remote_copy(
                    src_ref=win_ref.at[4, pl.ds(1 - half, 1)],
                    dst_ref=win_ref.at[8 - slot, pl.ds(2, 1)],
                    send_sem=win_send.at[9 + slot],
                    recv_sem=win_recv.at[9 + slot],
                    device_id=spatial(ds, dy, 1 - half),
                    device_id_type=MESH,
                )
            )
            window[-1].start()

    parts[node] = share[node]
    for copy in rs:
        copy.wait_recv()
    sums = parts[0]
    for n in range(1, nodes):
        sums = sums + parts[n]
    top_gram_ref[node] = sums[0:rows]
    top_moment_ref[...] = sums[rows : rows + 1]
    ag = []
    for k in range(1, nodes):
        ag.append(
            pltpu.make_async_remote_copy(
                src_ref=top_gram_ref.at[node],
                dst_ref=top_gram_ref.at[node],
                send_sem=ag_send.at[k],
                recv_sem=ag_recv.at[k],
                device_id=in_block(k),
                device_id_type=MESH,
            )
        )
        ag[-1].start()
    for copy in rs:
        copy.wait_send()
    for copy in window + ag:
        copy.wait()


def leaf_kernel(
    count_ref,
    near_ref,
    win_ref,
    gram_ref,
    moment_ref,
    top_gram_ref,
    top_moment_ref,
    near_out,
    coeffs_out,
    factor_out,
    top_coeffs_out,
    targets,
    weights,
    totals,
    work,
    upper,
):
    block = lax.axis_index("leaf")
    node = lax.axis_index("node")
    slab, y, half = place(node)
    size = win_ref.shape[3]
    rank = gram_ref.shape[1]
    centre = centre_of(block, node)

    row = lax.broadcasted_iota(jnp.int32, (32, near_ref.shape[1]), 0)
    lane = lax.broadcasted_iota(jnp.int32, (32, near_ref.shape[1]), 1)
    ids = jnp.full(row.shape, -1, jnp.int32)
    for k in range(27):
        ds, dy, w = k // 9 - 1, k // 3 % 3 - 1, k % 3
        z = 2 * half + w if w < 2 else 2 - half
        base = (2 * block + slab + ds) * ACROSS * ACROSS
        leaf = base + lax.rem(y + dy + ACROSS, ACROSS) * ACROSS + z
        ids = jnp.where(row == k, leaf, ids)
    for t in range(2):
        hit = (near_ref[t : t + 1, :] == ids) & (lane < count_ref[t])
        weight = jnp.sum(hit.astype(jnp.float32), 1, keepdims=True)
        own = row[:, 0:1] == 12 + t
        weights[t] = jnp.broadcast_to(jnp.where(own, 1.0, weight), (32, 128))
        targets[t] = target_features(centred(win_ref[4, t, 0:3, :], centre))
    totals[...] = jnp.zeros_like(totals)

    def add_tile(t, features, charges, source):
        weight = weights[t, pl.ds(source, 1), :]
        charges = charges * jnp.concatenate([weight] * (size // 128), 1)
        for c in range(size // CHUNK):
            chunk = slice(c * CHUNK, (c + 1) * CHUNK)
            distance = jnp.dot(targets[t, chunk, :], features, preferred_element_type=jnp.float32)
            terms = lax.rsqrt(distance) * charges
            total = terms[:, 0:128]
            for k in range(1, size // 128):
                total = total + terms[:, k * 128 : (k + 1) * 128]
            totals[t, chunk, :] += total

    @pl.loop(0, 9)
    def _(slot):
        for w in range(3):
            points = win_ref[slot, w]
            features = source_features(centred(points[0:3], centre))
            for t in (0, 1) if w < 2 else (1 - half,):
                add_tile(t, features, points[3:4], slot * 3 + w)

    for t in range(2):
        near = lax.dot_general(
            jnp.ones((8, 128), jnp.float32),
            totals[t],
            (((1,), (1,)), ((), ())),
            precision=HIGHEST,
            preferred_element_type=jnp.float32,
        )
        near_out[:, t * size : (t + 1) * size] = near[0:1]

    for i in range(3):
        if i < 2:
            work[i, :, 0:rank] = gram_ref[i]
            moment = moment_ref[i, 0:1, :]
        else:
            work[i, :, 0:rank] = top_gram_ref[...].reshape(rank, rank)
            moment = top_moment_ref[...]
        work[i, :, rank:] = jnp.broadcast_to(moment, (rank, rank)).T
    row = lax.broadcasted_iota(jnp.int32, (PANEL, rank), 0)
    col = lax.broadcasted_iota(jnp.int32, (PANEL, rank), 1)
    for low in range(0, rank, PANEL):
        high = low + PANEL
        for i in range(3):
            panel = work[i, low:high, 0:rank]
            right = work[i, low:high, rank:]
            columns = [
                jnp.broadcast_to(panel[:, low + j : low + j + 1], (PANEL, rank))
                for j in range(PANEL)
            ]
            done = jnp.zeros((PANEL, rank), jnp.float32)
            done_right = done
            for j in range(PANEL):
                inverse = lax.rsqrt(columns[j][j : j + 1, :])
                below = jnp.where(row > j, columns[j] * inverse, 0.0)
                pivot = panel[j : j + 1] * inverse
                pivot_right = right[j : j + 1] * inverse
                done = jnp.where(row == j, pivot, done)
                done_right = jnp.where(row == j, pivot_right, done_right)
                if j + 1 < PANEL:
                    panel = panel - below * pivot
                    right = right - below * pivot_right
                    for k in range(j + 1, PANEL):
                        columns[k] = columns[k] - below * (columns[k][j : j + 1, :] * inverse)
            done = jnp.where(col >= row + low, done, 0.0)
            upper[i, low:high, 0:rank] = done
            upper[i, low:high, rank:] = done_right
            if high < rank:
                a, b, c = split3(jnp.concatenate([done, done_right], 1))
                left = jnp.concatenate([a, b, c, a, b, a], 0)[:, 0:rank]
                both = jnp.concatenate([a, a, a, b, b, c], 0).astype(jnp.bfloat16)
                update = jnp.dot(
                    left.T.astype(jnp.bfloat16), both, preferred_element_type=jnp.float32
                )
                work[i, high:, :] = work[i, high:, :] - update[high:]

    full_row = lax.broadcasted_iota(jnp.int32, (rank, rank), 0)
    full_col = lax.broadcasted_iota(jnp.int32, (rank, rank), 1)
    for i in range(2):
        diagonal = jnp.where(full_row == full_col, upper[i, :, rank:], 0.0)
        coeffs_out[i : i + 1, :] = jnp.sum(diagonal, 0, keepdims=True)
    work[2, :, 0:rank] = upper[2, :, 0:rank].T
    rows = factor_out.shape[1]
    mine = pl.ds(pl.multiple_of(node * rows, rows), rows)
    factor_out[0] = work[2, mine, 0:rank]
    diagonal = jnp.where(
        full_row[0:rows] == full_col[0:rows], upper[2, mine, rank:], 0.0
    )
    top_coeffs_out[...] = jnp.sum(diagonal, 0, keepdims=True)[:, 0:rows]


def body(positions, charges, near_list, near_count, far_sample, proxies, strengths):
    blocks = lax.axis_size("leaf")
    nodes = lax.axis_size("node")
    size = charges.shape[0] // near_count.shape[0]
    rank = far_sample.shape[1]
    rows = rank // nodes
    vmem = pl.BlockSpec(memory_space=pltpu.VMEM)
    shape = lambda *dims: jax.ShapeDtypeStruct(dims, jnp.float32)
    window, gram, moment, top_gram, top_moment = pl.pallas_call(
        functools.partial(exchange_kernel, blocks, nodes),
        out_shape=(
            shape(9, 3, 4, size),
            shape(2, rank, rank),
            shape(2, 8, rank),
            shape(nodes, rows, rank),
            shape(1, rank),
        ),
        in_specs=[vmem] * 5,
        out_specs=(vmem,) * 5,
        scratch_shapes=[
            pltpu.VMEM((nodes, rows + 1, rank), jnp.float32),
            pltpu.VMEM((nodes, rows + 1, rank), jnp.float32),
            pltpu.SemaphoreType.DMA((18,)),
            pltpu.SemaphoreType.DMA((18,)),
            pltpu.SemaphoreType.DMA((nodes,)),
            pltpu.SemaphoreType.DMA((nodes,)),
            pltpu.SemaphoreType.DMA((nodes,)),
            pltpu.SemaphoreType.DMA((nodes,)),
        ],
        compiler_params=pltpu.CompilerParams(collective_id=0, has_side_effects=True),
        name="exchange",
    )(positions, charges[None, :], far_sample, proxies, strengths)
    smem = pl.BlockSpec(memory_space=pltpu.SMEM)
    near, coeffs, factor, top_coeffs = pl.pallas_call(
        leaf_kernel,
        out_shape=(shape(1, 2 * size), shape(2, rank), shape(1, rows, rank), shape(1, rows)),
        in_specs=[smem] + [vmem] * 6,
        out_specs=(vmem,) * 4,
        scratch_shapes=[
            pltpu.VMEM((2, size, 64), jnp.bfloat16),
            pltpu.VMEM((2, 32, 128), jnp.float32),
            pltpu.VMEM((2, size, 128), jnp.float32),
            pltpu.VMEM((3, rank, 2 * rank), jnp.float32),
            pltpu.VMEM((3, rank, 2 * rank), jnp.float32),
        ],
        name="leaf",
    )(near_count, near_list, window, gram, moment, top_gram, top_moment)
    return (near.reshape(-1), coeffs, factor, top_coeffs)


def solution(mesh):
    in_specs = (
        P(None, ("leaf", "node")),
        P(("leaf", "node")),
        P(("leaf", "node"), None),
        P(("leaf", "node")),
        P(("leaf", "node"), None),
        P(("leaf", "node"), None, None),
        P(("leaf", "node"), None),
    )
    out_specs = (
        P(("leaf", "node")),
        P(("leaf", "node"), None),
        P("leaf", "node", None),
        P("leaf", "node"),
    )
    return jax.shard_map(body, mesh=mesh, in_specs=in_specs, out_specs=out_specs, check_vma=False)
```

time: 388 us -> 48.2 us (0.12)
  the two profiles are of different devices: /device:TPU:160 before, /device:TPU:1 now
where the time goes in v1:
time: 48.2 us; the launch traced here: 47.9 us
  Pallas kernels  46 us (95%)
  local copies, waits for them, and re-layouts  1.28 us (3%)
  between operations  0.64 us (1%)
    pallas_call x1, Pallas kernels, body(): pl.pallas_call(functools.partial(exchange_kernel, blocks, nodes), out_sha...  31.1 us
    pallas_call x1, Pallas kernels, body(): pl.pallas_call(leaf_kernel, out_shape=(shape(1, 2 * size), shape(2, rank)...  14.9 us
    unnamed x1, local copies, waits for them, and re-layouts  1.28 us

profile of v1, /device:TPU:1, one launch (start us, length us, event | category | flops | bytes accessed | tf_op | source)
XLA Modules:
  0.0 47.9 jit_solution(13510119987445093476)
XLA Ops:
  0.6 1.3 %copy.11.proxy_ref = f32[2,3,128]{2,1,0:T(4,128)} copy(f32[2,3,128]{2,0,1:T(2,128)} %param.12) | data formatting | bytes 6144 | tf_op args[5]
  1.9 31.1 %exchange.1 = (f32[9,3,4,512]{3,2,1,0:T(4,128)}, f32[2,128,128]{2,1,0:T(8,128)}, f32[2,8,128]{2,1,0:T(8,128)}, f32[16,8,128]{2,1,0:T(8,128)}, f32[1,128]{1,0:T(1,128)}) custom-call(f32[3,1024]{1,0:T(4,128)} %pos_ref.1, f32[1,1024]{1,0:T(1,128)} %bitcast.2, f32[1024,128]{1,0:T(8,128)} %far_ref.1, f32[2,3,128]{2,1,0:T(4,128)} %copy.11.proxy_ref, ...), custom_call_target="tpu_custom_call" | custom-call | tf_op jit(solution)/shard_map/exchange/pallas_call | solution.py:357
  33.0 14.9 %leaf.1 = (f32[1,1024]{1,0:T(1,128)}, f32[2,128]{1,0:T(2,128)}, f32[1,8,128]{2,1,0:T(8,128)}, f32[1,8]{1,0:T(1,128)}) custom-call(s32[2]{0:T(128)} %count_ref.1, s32[2,26]{1,0:T(2,128)} %near_ref.1, f32[9,3,4,512]{3,2,1,0:T(4,128)} %get-tuple-element.13.win_ref, f32[2,128,128]{2,1,0:T(8,128)} %get-tuple-element.14.gram_ref, ...), custom_call_target="tpu_custom_call" | custom-call | tf_op jit(solution)/shard_map/leaf/pallas_call | solution.py:382

commit v2 on v1

v2 whole, which is shorter than its diff:
```python
import functools

import jax
import jax.numpy as jnp
from jax import lax
from jax.experimental import pallas as pl
from jax.experimental.pallas import tpu as pltpu
from jax.sharding import PartitionSpec as P

soft_square = 0.0025
ACROSS = 4
PANEL = 16
MESH = pl.DeviceIdType.MESH
HIGHEST = lax.Precision.HIGHEST


def split3(v):
    high = v.astype(jnp.bfloat16).astype(jnp.float32)
    rest = v - high
    mid = rest.astype(jnp.bfloat16).astype(jnp.float32)
    return high, mid, rest - mid


def feature_rows(xyz, fourth, fifth):
    row = lax.broadcasted_iota(jnp.int32, (8, xyz.shape[1]), 0)
    rows = jnp.where(row == 4, fifth, 0.0)
    rows = jnp.where(row == 3, fourth, rows)
    for k in range(3):
        rows = jnp.where(row == k, xyz[k : k + 1], rows)
    return split3(rows)


def source_features(xyz):
    high, mid, low = feature_rows(xyz, jnp.sum(xyz * xyz, 0, keepdims=True), 1.0)
    return jnp.concatenate([high, high, high, mid, mid, mid, low, low], 0).astype(jnp.bfloat16)


def target_features(xyz):
    norm = jnp.sum(xyz * xyz, 0, keepdims=True) + soft_square
    high, mid, low = feature_rows(-2.0 * xyz, 1.0, norm)
    return jnp.concatenate([high, mid, low, high, mid, low, high, mid], 0).T.astype(jnp.bfloat16)


def place(node):
    return node // 8, lax.rem(node // 2, ACROSS), lax.rem(node, 2)


def centre_of(block, node):
    slab, y, half = place(node)
    return (
        (2 * block + slab).astype(jnp.float32) + 0.5,
        y.astype(jnp.float32) + 0.5,
        (2 * half).astype(jnp.float32) + 1.0,
    )


def centred(rows, centre):
    row = lax.broadcasted_iota(jnp.int32, rows.shape, 0)
    shift = jnp.where(row == 0, centre[0], jnp.where(row == 1, centre[1], centre[2]))
    return rows - shift


def read_weights(block, node, near_ref, count_ref, weights):
    slab, y, half = place(node)
    row = lax.broadcasted_iota(jnp.int32, (32, near_ref.shape[1]), 0)
    lane = lax.broadcasted_iota(jnp.int32, (32, near_ref.shape[1]), 1)
    ids = jnp.full(row.shape, -1, jnp.int32)
    for k in range(27):
        ds, dy, w = k // 9 - 1, k // 3 % 3 - 1, k % 3
        z = 2 * half + w if w < 2 else 2 - half
        base = (2 * block + slab + ds) * ACROSS * ACROSS
        leaf = base + lax.rem(y + dy + ACROSS, ACROSS) * ACROSS + z
        ids = jnp.where(row == k, leaf, ids)
    for t in range(2):
        hit = (near_ref[t : t + 1, :] == ids) & (lane < count_ref[t])
        weight = jnp.sum(jnp.where(hit, 1.0, 0.0), 1, keepdims=True)
        own = row[:, 0:1] == 12 + t
        weights[t] = jnp.broadcast_to(jnp.where(own, 1.0, weight), (32, 128))


def add_tile(t, features, charges, weight, targets, totals):
    size = charges.shape[1]
    charges = charges * jnp.concatenate([weight] * (size // 128), 1)
    distance = jnp.dot(targets[t], features, preferred_element_type=jnp.float32)
    terms = lax.rsqrt(distance) * charges
    total = terms[:, 0:128]
    for k in range(1, size // 128):
        total = total + terms[:, k * 128 : (k + 1) * 128]
    totals[t] += total


def lane_sums(totals):
    ones = jnp.ones((8, totals.shape[1]), jnp.float32)
    return lax.dot_general(
        ones, totals, (((1,), (1,)), ((), ())), precision=HIGHEST, preferred_element_type=jnp.float32
    )[0:1]


def factorize(work, upper):
    count, rank = work.shape[0], work.shape[1]
    row = lax.broadcasted_iota(jnp.int32, (count, PANEL, rank), 1)
    col = lax.broadcasted_iota(jnp.int32, (count, PANEL, rank), 2)
    for low in range(0, rank, PANEL):
        high = low + PANEL
        panel = work[:, low:high, 0:rank]
        right = work[:, low:high, rank:]
        columns = [
            jnp.broadcast_to(panel[:, :, low + j : low + j + 1], (count, PANEL, rank))
            for j in range(PANEL)
        ]
        done = jnp.zeros((count, PANEL, rank), jnp.float32)
        done_right = done
        for j in range(PANEL):
            inverse = lax.rsqrt(columns[j][:, j : j + 1, :])
            below = jnp.where(row > j, columns[j] * inverse, 0.0)
            pivot = panel[:, j : j + 1] * inverse
            pivot_right = right[:, j : j + 1] * inverse
            done = jnp.where(row == j, pivot, done)
            done_right = jnp.where(row == j, pivot_right, done_right)
            if j + 1 < PANEL:
                panel = panel - below * pivot
                right = right - below * pivot_right
                for k in range(j + 1, PANEL):
                    columns[k] = columns[k] - below * (columns[k][:, j : j + 1, :] * inverse)
        done = jnp.where(col >= row + low, done, 0.0)
        upper[:, low:high, 0:rank] = done
        upper[:, low:high, rank:] = done_right
        if high < rank:
            for i in range(count):
                a, b, c = split3(jnp.concatenate([done[i], done_right[i]], 1))
                left = jnp.concatenate([a, b, c, a, b, a], 0)[:, 0:rank]
                both = jnp.concatenate([a, a, a, b, b, c], 0).astype(jnp.bfloat16)
                update = jnp.dot(
                    left.T.astype(jnp.bfloat16), both, preferred_element_type=jnp.float32
                )
                work[i, high:, :] = work[i, high:, :] - update[high:]


def diagonal_row(columns):
    row = lax.broadcasted_iota(jnp.int32, columns.shape, 0)
    col = lax.broadcasted_iota(jnp.int32, columns.shape, 1)
    return jnp.sum(jnp.where(row == col, columns, 0.0), 0, keepdims=True)


def exchange_kernel(
    blocks,
    nodes,
    count_ref,
    near_ref,
    pos_ref,
    charge_ref,
    far_ref,
    proxy_ref,
    strength_ref,
    near_out,
    coeffs_out,
    top_gram_ref,
    top_moment_ref,
    win_ref,
    targets,
    weights,
    totals,
    work,
    upper,
    share,
    parts,
    win_send,
    win_recv,
    rs_send,
    rs_recv,
    ag_send,
    ag_recv,
):
    block = lax.axis_index("leaf")
    node = lax.axis_index("node")
    slab, y, half = place(node)
    size = pos_ref.shape[1] // 2
    rank = far_ref.shape[1]

    def spatial(ds, dy, core):
        level = slab + ds
        step = (level + 2) // 2 - 1
        level = level - 2 * step
        other = level * 8 + lax.rem(y + dy + ACROSS, ACROSS) * 2 + core
        return (lax.rem(block + step + blocks, blocks), other)

    def in_block(k):
        return (block, lax.rem(node + k, nodes))

    outside = 1 - 2 * slab
    barrier = pltpu.get_barrier_semaphore()
    for k in range(1, nodes):
        pl.semaphore_signal(barrier, inc=1, device_id=in_block(k), device_id_type=MESH)
    for dy in (-1, 0, 1):
        for core in (0, 1):
            target = spatial(-outside, dy, core)
            pl.semaphore_signal(barrier, inc=1, device_id=target, device_id_type=MESH)

    for t in range(2):
        lanes = slice(t * size, (t + 1) * size)
        win_ref[4, t, 0:3, :] = pos_ref[:, lanes]
        win_ref[4, t, 3:4, :] = charge_ref[:, lanes]
    centre = centre_of(block, node)
    for t in range(2):
        lanes = slice(t * size, (t + 1) * size)
        targets[t] = target_features(centred(pos_ref[:, lanes], centre))
        distance = jnp.dot(
            targets[t],
            source_features(centred(proxy_ref[:, t, :], centre)),
            preferred_element_type=jnp.float32,
        )
        response = far_ref[lanes, :] + lax.rsqrt(distance) * strength_ref[t : t + 1, :]
        gram = lax.dot_general(
            response,
            response,
            (((0,), (0,)), ((), ())),
            precision=HIGHEST,
            preferred_element_type=jnp.float32,
        )
        moment = jnp.dot(
            jnp.broadcast_to(charge_ref[:, lanes], (8, size)),
            response,
            precision=HIGHEST,
            preferred_element_type=jnp.float32,
        )[0:1]
        work[t, :, 0:rank] = gram
        total = gram if t == 0 else total + gram
        total_moment = moment if t == 0 else total_moment + moment
        work[t, :, rank:] = jnp.broadcast_to(moment, (rank, rank)).T
    rows = rank // nodes
    for n in range(nodes):
        share[n, 0:rows, :] = total[n * rows : (n + 1) * rows]
        share[n, rows : rows + 1, :] = total_moment

    pl.semaphore_wait(barrier, nodes - 1 + 6)

    rs = []
    for k in range(1, nodes):
        target = in_block(k)
        rs.append(
            pltpu.make_async_remote_copy(
                src_ref=share.at[target[1]],
                dst_ref=parts.at[node],
                send_sem=rs_send.at[k],
                recv_sem=rs_recv.at[k],
                device_id=target,
                device_id_type=MESH,
            )
        )
        rs[-1].start()
    window = {}
    for ds in (-1, 0, 1):
        for dy in (-1, 0, 1):
            slot = 4 + 3 * ds + dy
            if slot != 4:
                window[slot, 0] = (
                    pltpu.make_async_remote_copy(
                        src_ref=win_ref.at[4, pl.ds(0, 2)],
                        dst_ref=win_ref.at[8 - slot, pl.ds(0, 2)],
                        send_sem=win_send.at[slot],
                        recv_sem=win_recv.at[slot],
                        device_id=spatial(ds, dy, half),
                        device_id_type=MESH,
                    )
                )
                window[slot, 0].start()
            window[slot, 1] = (
                pltpu.make_async_remote_copy(
                    src_ref=win_ref.at[4, pl.ds(1 - half, 1)],
                    dst_ref=win_ref.at[8 - slot, pl.ds(2, 1)],
                    send_sem=win_send.at[9 + slot],
                    recv_sem=win_recv.at[9 + slot],
                    device_id=spatial(ds, dy, 1 - half),
                    device_id_type=MESH,
                )
            )
            window[slot, 1].start()

    parts[node] = share[node]

    factorize(work, upper)
    for i in range(2):
        coeffs_out[i : i + 1, :] = diagonal_row(upper[i, :, rank:])
    read_weights(block, node, near_ref, count_ref, weights)
    totals[...] = jnp.zeros_like(totals)

    def add_source(slot, w):
        points = win_ref[slot, w]
        features = source_features(centred(points[0:3], centre))
        for t in (0, 1) if w < 2 else (1 - half,):
            k = slot * 3 + w
            add_tile(t, features, points[3:4], weights[t, k : k + 1, :], targets, totals)

    for w in range(2):
        add_source(4, w)

    for copy in rs:
        copy.wait_recv()
    sums = parts[0]
    for n in range(1, nodes):
        sums = sums + parts[n]
    top_gram_ref[node] = sums[0:rows]
    top_moment_ref[...] = sums[rows : rows + 1]
    ag = []
    for k in range(1, nodes):
        ag.append(
            pltpu.make_async_remote_copy(
                src_ref=top_gram_ref.at[node],
                dst_ref=top_gram_ref.at[node],
                send_sem=ag_send.at[k],
                recv_sem=ag_recv.at[k],
                device_id=in_block(k),
                device_id_type=MESH,
            )
        )
        ag[-1].start()

    for group in ((4, 3, 5), (0, 1, 2), (6, 7, 8)):
        for slot in group:
            for part in (0, 1):
                if (slot, part) in window:
                    window[8 - slot, part].wait_recv()
        for slot in group:
            for w in (2,) if slot == 4 else (0, 1, 2):
                add_source(slot, w)
    for t in range(2):
        near_out[:, t * size : (t + 1) * size] = lane_sums(totals[t])
    for copy in rs + list(window.values()):
        copy.wait_send()
    for copy in ag:
        copy.wait()


def top_kernel(
    near_ref,
    coeffs_ref,
    gram_ref,
    moment_ref,
    near_out,
    coeffs_out,
    factor_out,
    top_coeffs_out,
    work,
    upper,
):
    node = lax.axis_index("node")
    rank = work.shape[1]
    near_out[...] = near_ref[...]
    coeffs_out[...] = coeffs_ref[...]
    work[0, :, 0:rank] = gram_ref[...].reshape(rank, rank)
    work[0, :, rank:] = jnp.broadcast_to(moment_ref[...], (rank, rank)).T
    factorize(work, upper)
    work[0, :, 0:rank] = upper[0, :, 0:rank].T
    rows = factor_out.shape[1]
    mine = pl.ds(pl.multiple_of(node * rows, rows), rows)
    factor_out[0] = work[0, mine, 0:rank]
    top_coeffs_out[...] = diagonal_row(upper[0, mine, rank:])[:, 0:rows]


def body(positions, charges, near_list, near_count, far_sample, proxies, strengths):
    blocks = lax.axis_size("leaf")
    nodes = lax.axis_size("node")
    size = charges.shape[0] // near_count.shape[0]
    rank = far_sample.shape[1]
    rows = rank // nodes
    vmem = pl.BlockSpec(memory_space=pltpu.VMEM)
    smem = pl.BlockSpec(memory_space=pltpu.SMEM)
    shape = lambda *dims: jax.ShapeDtypeStruct(dims, jnp.float32)
    scratch = lambda *dims: pltpu.VMEM(dims, jnp.float32)
    semaphores = lambda n: pltpu.SemaphoreType.DMA((n,))
    near, coeffs, top_gram, top_moment = pl.pallas_call(
        functools.partial(exchange_kernel, blocks, nodes),
        out_shape=(
            shape(1, 2 * size),
            shape(2, rank),
            shape(nodes, rows, rank),
            shape(1, rank),
        ),
        in_specs=[smem] + [vmem] * 6,
        out_specs=(vmem,) * 4,
        scratch_shapes=[
            scratch(9, 3, 4, size),
            pltpu.VMEM((2, size, 64), jnp.bfloat16),
            scratch(2, 32, 128),
            scratch(2, size, 128),
            scratch(2, rank, 2 * rank),
            scratch(2, rank, 2 * rank),
            scratch(nodes, rows + 1, rank),
            scratch(nodes, rows + 1, rank),
            semaphores(18),
            semaphores(18),
            semaphores(nodes),
            semaphores(nodes),
            semaphores(nodes),
            semaphores(nodes),
        ],
        compiler_params=pltpu.CompilerParams(collective_id=0, has_side_effects=True),
        name="exchange",
    )(
        near_count,
        near_list,
        positions,
        charges[None, :],
        far_sample,
        jnp.transpose(proxies, (1, 0, 2)),
        strengths,
    )
    near, coeffs, factor, top_coeffs = pl.pallas_call(
        top_kernel,
        out_shape=(shape(1, 2 * size), shape(2, rank), shape(1, rows, rank), shape(1, rows)),
        in_specs=[vmem] * 4,
        out_specs=(vmem,) * 4,
        scratch_shapes=[scratch(1, rank, 2 * rank)] * 2,
        name="top",
    )(near, coeffs, top_gram, top_moment)
    return (near.reshape(-1), coeffs, factor, top_coeffs)


def solution(mesh):
    in_specs = (
        P(None, ("leaf", "node")),
        P(("leaf", "node")),
        P(("leaf", "node"), None),
        P(("leaf", "node")),
        P(("leaf", "node"), None),
        P(("leaf", "node"), None, None),
        P(("leaf", "node"), None),
    )
    out_specs = (
        P(("leaf", "node")),
        P(("leaf", "node"), None),
        P("leaf", "node", None),
        P("leaf", "node"),
    )
    return jax.shard_map(body, mesh=mesh, in_specs=in_specs, out_specs=out_specs, check_vma=False)
```

time: 48.2 us -> 43.3 us (0.90)
  Pallas kernels: 46 us -> 42.4 us
  local copies, waits for them, and re-layouts: 1.28 us -> 0 us
    pallas_call x1, Pallas kernels: 14.9 us -> 4.95 us  [body(): pl.pallas_call(top_kernel, out_shape=(shape(1, 2 * size), shape(2, rank),...]
    pallas_call x1, Pallas kernels: 31.1 us -> 37.5 us  [body(): pl.pallas_call(functools.partial(exchange_kernel, blocks, nodes), out_sha...]
    unnamed x1 -> x0, local copies, waits for them, and re-layouts: 1.28 us -> none
where the time goes in v2:
time: 43.3 us; the launch traced here: 43.1 us
  Pallas kernels  42.4 us (98%)
  between operations  0.64 us (1%)
    pallas_call x1, Pallas kernels, body(): pl.pallas_call(functools.partial(exchange_kernel, blocks, nodes), out_sha...  37.5 us
    pallas_call x1, Pallas kernels, body(): pl.pallas_call(top_kernel, out_shape=(shape(1, 2 * size), shape(2, rank),...  4.95 us

profile of v2, /device:TPU:1, one launch (start us, length us, event | category | flops | bytes accessed | tf_op | source)
XLA Modules:
  0.0 43.1 jit_solution(261368084933500403)
XLA Ops:
  0.6 37.5 %exchange.1 = (f32[1,1024]{1,0:T(1,128)}, f32[2,128]{1,0:T(2,128)}, f32[16,8,128]{2,1,0:T(8,128)}, f32[1,128]{1,0:T(1,128)}) custom-call(s32[2]{0:T(128)} %count_ref.1, s32[2,26]{1,0:T(2,128)} %near_ref.1, f32[3,1024]{1,0:T(4,128)} %pos_ref.1, f32[1,1024]{1,0:T(1,128)} %bitcast.3, f32[1024,128]{1,0:T(8,128)} %far_ref.1, f32[3,2,128]{2,1,0:T(2,128)} %bitcast.4, ...), custom_call_target="tpu_custom_call" | custom-call | tf_op jit(solution)/shard_map/exchange/pallas_call | solution.py:371
  38.1 5.0 %top.1 = (f32[1,1024]{1,0:T(1,128)}, f32[2,128]{1,0:T(2,128)}, f32[1,8,128]{2,1,0:T(8,128)}, f32[1,8]{1,0:T(1,128)}) custom-call(f32[1,1024]{1,0:T(1,128)} %get-tuple-element.12.near_ref, f32[2,128]{1,0:T(2,128)} %get-tuple-element.13.coeffs_ref, f32[16,8,128]{2,1,0:T(8,128)} %get-tuple-element.14.gram_ref, f32[1,128]{1,0:T(1,128)} %get-tuple-element.15.moment_ref), custom_call_target="tpu_custom_call" | custom-call | tf_op jit(solution)/shard_map/top/pallas_call | solution.py:408

commit v3 on v2

--- a/solution.py
+++ b/solution.py
@@ -10,8 +10,11 @@
 soft_square = 0.0025
 ACROSS = 4
 PANEL = 16
+PIECE = 128
 MESH = pl.DeviceIdType.MESH
 HIGHEST = lax.Precision.HIGHEST
+EARLY = 6
+GROUPS = ((3, 5), (0, 1, 2), (6, 7, 8))
 
 
 def split3(v):
@@ -78,15 +81,26 @@
         weights[t] = jnp.broadcast_to(jnp.where(own, 1.0, weight), (32, 128))
 
 
-def add_tile(t, features, charges, weight, targets, totals):
-    size = charges.shape[1]
-    charges = charges * jnp.concatenate([weight] * (size // 128), 1)
-    distance = jnp.dot(targets[t], features, preferred_element_type=jnp.float32)
-    terms = lax.rsqrt(distance) * charges
-    total = terms[:, 0:128]
-    for k in range(1, size // 128):
-        total = total + terms[:, k * 128 : (k + 1) * 128]
-    totals[t] += total
+def near_work(sources, half, centre, win_ref, weights, targets, totals):
+    size = win_ref.shape[3]
+
+    def piece(t, rows, features, charges):
+        distance = jnp.dot(targets[t, rows, :], features, preferred_element_type=jnp.float32)
+        terms = lax.rsqrt(distance) * charges
+        total = terms[:, 0:128]
+        for k in range(1, size // 128):
+            total = total + terms[:, k * 128 : (k + 1) * 128]
+        totals[t, rows, :] += total
+
+    for slot, w in sources:
+        points = win_ref[slot, w]
+        features = source_features(centred(points[0:3], centre))
+        for t in (0, 1) if w < 2 else (1 - half,):
+            weight = weights[t, slot * 3 + w : slot * 3 + w + 1, :]
+            charges = points[3:4] * jnp.concatenate([weight] * (size // 128), 1)
+            for start in range(0, size, PIECE):
+                piece(t, slice(start, start + PIECE), features, charges)
+                yield
 
 
 def lane_sums(totals):
@@ -96,11 +110,14 @@
     )[0:1]
 
 
-def factorize(work, upper):
+def factorize(work, upper, panels, other=(), pieces=0):
+    other = iter(other)
+    pivots = len(panels) * PANEL
+    steps = 0
     count, rank = work.shape[0], work.shape[1]
     row = lax.broadcasted_iota(jnp.int32, (count, PANEL, rank), 1)
     col = lax.broadcasted_iota(jnp.int32, (count, PANEL, rank), 2)
-    for low in range(0, rank, PANEL):
+    for low in (p * PANEL for p in panels):
         high = low + PANEL
         panel = work[:, low:high, 0:rank]
         right = work[:, low:high, rank:]
@@ -111,6 +128,9 @@
         done = jnp.zeros((count, PANEL, rank), jnp.float32)
         done_right = done
         for j in range(PANEL):
+            for _ in range(pieces * steps // pivots, pieces * (steps + 1) // pivots):
+                next(other)
+            steps += 1
             inverse = lax.rsqrt(columns[j][:, j : j + 1, :])
             below = jnp.where(row > j, columns[j] * inverse, 0.0)
             pivot = panel[:, j : j + 1] * inverse
@@ -149,7 +169,7 @@
     near_ref,
     pos_ref,
     charge_ref,
-    far_ref,
+    far_hbm,
     proxy_ref,
     strength_ref,
     near_out,
@@ -157,13 +177,15 @@
     top_gram_ref,
     top_moment_ref,
     win_ref,
+    weights,
+    far_ref,
     targets,
-    weights,
     totals,
     work,
     upper,
     share,
     parts,
+    far_sem,
     win_send,
     win_recv,
     rs_send,
@@ -187,6 +209,14 @@
     def in_block(k):
         return (block, lax.rem(node + k, nodes))
 
+    far_copies = []
+    for t in range(2):
+        lanes = pl.ds(t * size, size)
+        far_copies.append(
+            pltpu.make_async_copy(far_hbm.at[lanes], far_ref.at[lanes], far_sem.at[t])
+        )
+        far_copies[t].start()
+
     outside = 1 - 2 * slab
     barrier = pltpu.get_barrier_semaphore()
     for k in range(1, nodes):
@@ -209,6 +239,7 @@
             source_features(centred(proxy_ref[:, t, :], centre)),
             preferred_element_type=jnp.float32,
         )
+        far_copies[t].wait()
         response = far_ref[lanes, :] + lax.rsqrt(distance) * strength_ref[t : t + 1, :]
         gram = lax.dot_general(
             response,
@@ -249,50 +280,44 @@
         )
         rs[-1].start()
     window = {}
-    for ds in (-1, 0, 1):
+    for ds in (-1, 1, 0):
         for dy in (-1, 0, 1):
             slot = 4 + 3 * ds + dy
             if slot != 4:
-                window[slot, 0] = (
-                    pltpu.make_async_remote_copy(
-                        src_ref=win_ref.at[4, pl.ds(0, 2)],
-                        dst_ref=win_ref.at[8 - slot, pl.ds(0, 2)],
-                        send_sem=win_send.at[slot],
-                        recv_sem=win_recv.at[slot],
-                        device_id=spatial(ds, dy, half),
-                        device_id_type=MESH,
-                    )
-                )
-                window[slot, 0].start()
-            window[slot, 1] = (
-                pltpu.make_async_remote_copy(
-                    src_ref=win_ref.at[4, pl.ds(1 - half, 1)],
-                    dst_ref=win_ref.at[8 - slot, pl.ds(2, 1)],
-                    send_sem=win_send.at[9 + slot],
-                    recv_sem=win_recv.at[9 + slot],
-                    device_id=spatial(ds, dy, 1 - half),
+                window[8 - slot] = pltpu.make_async_remote_copy(
+                    src_ref=win_ref.at[4, pl.ds(0, 2)],
+                    dst_ref=win_ref.at[8 - slot, pl.ds(0, 2)],
+                    send_sem=win_send.at[8 - slot],
+                    recv_sem=win_recv.at[8 - slot],
+                    device_id=spatial(ds, dy, half),
                     device_id_type=MESH,
                 )
-            )
-            window[slot, 1].start()
-
+                window[8 - slot].start()
+
+    forwards = {}
+
+    def forward(slot):
+        forwards[slot] = pltpu.make_async_remote_copy(
+            src_ref=win_ref.at[slot, pl.ds(1 - half, 1)],
+            dst_ref=win_ref.at[slot, pl.ds(2, 1)],
+            send_sem=win_send.at[9 + slot],
+            recv_sem=win_recv.at[9 + slot],
+            device_id=(block, node + 1 - 2 * half),
+            device_id_type=MESH,
+        )
+        forwards[slot].start()
+
+    forward(4)
     parts[node] = share[node]
 
-    factorize(work, upper)
-    for i in range(2):
-        coeffs_out[i : i + 1, :] = diagonal_row(upper[i, :, rank:])
     read_weights(block, node, near_ref, count_ref, weights)
     totals[...] = jnp.zeros_like(totals)
 
-    def add_source(slot, w):
-        points = win_ref[slot, w]
-        features = source_features(centred(points[0:3], centre))
-        for t in (0, 1) if w < 2 else (1 - half,):
-            k = slot * 3 + w
-            add_tile(t, features, points[3:4], weights[t, k : k + 1, :], targets, totals)
-
-    for w in range(2):
-        add_source(4, w)
+    def near(sources):
+        return near_work(sources, half, centre, win_ref, weights, targets, totals)
+
+    panels = range(rank // PANEL)
+    factorize(work, upper, panels[:EARLY], near([(4, 0), (4, 1)]), 4 * (size // PIECE))
 
     for copy in rs:
         copy.wait_recv()
@@ -315,17 +340,30 @@
         )
         ag[-1].start()
 
-    for group in ((4, 3, 5), (0, 1, 2), (6, 7, 8)):
+    late = (4,)
+    for group in GROUPS:
         for slot in group:
-            for part in (0, 1):
-                if (slot, part) in window:
-                    window[8 - slot, part].wait_recv()
-        for slot in group:
-            for w in (2,) if slot == 4 else (0, 1, 2):
-                add_source(slot, w)
+            window[slot].wait_recv()
+            forward(slot)
+        for slot in late:
+            forwards[slot].wait_recv()
+        sources = [(slot, 2) for slot in late]
+        if group != GROUPS[-1]:
+            sources += [(slot, w) for slot in group for w in range(2)]
+        work_left = near(sources)
+        if group == GROUPS[0]:
+            tiles = len(late) + 4 * len(group)
+            factorize(work, upper, panels[EARLY:], work_left, tiles * (size // PIECE))
+            for i in range(2):
+                coeffs_out[i : i + 1, :] = diagonal_row(upper[i, :, rank:])
+        for _ in work_left:
+            pass
+        late = group
     for t in range(2):
         near_out[:, t * size : (t + 1) * size] = lane_sums(totals[t])
-    for copy in rs + list(window.values()):
+    for slot in late:
+        forwards[slot].wait_recv()
+    for copy in rs + list(window.values()) + list(forwards.values()):
         copy.wait_send()
     for copy in ag:
         copy.wait()
@@ -336,20 +374,37 @@
     coeffs_ref,
     gram_ref,
     moment_ref,
+    win_ref,
+    weights,
     near_out,
     coeffs_out,
     factor_out,
     top_coeffs_out,
+    targets,
+    totals,
     work,
     upper,
 ):
+    block = lax.axis_index("leaf")
     node = lax.axis_index("node")
+    half = place(node)[2]
+    centre = centre_of(block, node)
     rank = work.shape[1]
-    near_out[...] = near_ref[...]
+    size = win_ref.shape[3]
+    for t in range(2):
+        targets[t] = target_features(centred(win_ref[4, t, 0:3, :], centre))
+    totals[...] = jnp.zeros_like(totals)
+    sources = [(slot, w) for slot in GROUPS[-1] for w in range(3)]
+    near = near_work(sources, half, centre, win_ref, weights, targets, totals)
+    pieces = 5 * len(GROUPS[-1]) * (size // PIECE)
+
     coeffs_out[...] = coeffs_ref[...]
     work[0, :, 0:rank] = gram_ref[...].reshape(rank, rank)
     work[0, :, rank:] = jnp.broadcast_to(moment_ref[...], (rank, rank)).T
-    factorize(work, upper)
+    factorize(work, upper, range(rank // PANEL), near, pieces)
+    for t in range(2):
+        lanes = slice(t * size, (t + 1) * size)
+        near_out[:, lanes] = near_ref[:, lanes] + lane_sums(totals[t])
     work[0, :, 0:rank] = upper[0, :, 0:rank].T
     rows = factor_out.shape[1]
     mine = pl.ds(pl.multiple_of(node * rows, rows), rows)
@@ -368,25 +423,27 @@
     shape = lambda *dims: jax.ShapeDtypeStruct(dims, jnp.float32)
     scratch = lambda *dims: pltpu.VMEM(dims, jnp.float32)
     semaphores = lambda n: pltpu.SemaphoreType.DMA((n,))
-    near, coeffs, top_gram, top_moment = pl.pallas_call(
+    near, coeffs, top_gram, top_moment, window, weights = pl.pallas_call(
         functools.partial(exchange_kernel, blocks, nodes),
         out_shape=(
             shape(1, 2 * size),
             shape(2, rank),
             shape(nodes, rows, rank),
             shape(1, rank),
+            shape(9, 3, 4, size),
+            shape(2, 32, 128),
         ),
-        in_specs=[smem] + [vmem] * 6,
-        out_specs=(vmem,) * 4,
+        in_specs=[smem] + [vmem] * 3 + [pl.BlockSpec(memory_space=pl.ANY)] + [vmem] * 2,
+        out_specs=(vmem,) * 6,
         scratch_shapes=[
-            scratch(9, 3, 4, size),
+            scratch(2 * size, rank),
             pltpu.VMEM((2, size, 64), jnp.bfloat16),
-            scratch(2, 32, 128),
             scratch(2, size, 128),
             scratch(2, rank, 2 * rank),
             scratch(2, rank, 2 * rank),
             scratch(nodes, rows + 1, rank),
             scratch(nodes, rows + 1, rank),
+            semaphores(2),
             semaphores(18),
             semaphores(18),
             semaphores(nodes),
@@ -408,11 +465,16 @@
     near, coeffs, factor, top_coeffs = pl.pallas_call(
         top_kernel,
         out_shape=(shape(1, 2 * size), shape(2, rank), shape(1, rows, rank), shape(1, rows)),
-        in_specs=[vmem] * 4,
+        in_specs=[vmem] * 6,
         out_specs=(vmem,) * 4,
-        scratch_shapes=[scratch(1, rank, 2 * rank)] * 2,
+        scratch_shapes=[
+            pltpu.VMEM((2, size, 64), jnp.bfloat16),
+            scratch(2, size, 128),
+            scratch(1, rank, 2 * rank),
+            scratch(1, rank, 2 * rank),
+        ],
         name="top",
-    )(near, coeffs, top_gram, top_moment)
+    )(near, coeffs, top_gram, top_moment, window, weights)
     return (near.reshape(-1), coeffs, factor, top_coeffs)
 
 

time: 43.3 us -> 38.2 us (0.88)
  Pallas kernels: 42.4 us -> 37.3 us
    pallas_call x1, Pallas kernels: 37.5 us -> 30.7 us  [body(): pl.pallas_call(functools.partial(exchange_kernel, blocks, nodes), out_sha...]
    pallas_call x1, Pallas kernels: 4.95 us -> 6.62 us  [body(): pl.pallas_call(top_kernel, out_shape=(shape(1, 2 * size), shape(2, rank),...]
where the time goes in v3:
time: 38.2 us; the launch traced here: 37.9 us
  Pallas kernels  37.3 us (98%)
  between operations  0.64 us (2%)
    pallas_call x1, Pallas kernels, body(): pl.pallas_call(functools.partial(exchange_kernel, blocks, nodes), out_sha...  30.7 us
    pallas_call x1, Pallas kernels, body(): pl.pallas_call(top_kernel, out_shape=(shape(1, 2 * size), shape(2, rank),...  6.62 us

profile of v3, /device:TPU:1, one launch (start us, length us, event | category | flops | bytes accessed | tf_op | source)
XLA Modules:
  0.0 37.9 jit_solution(18280267364669003048)
XLA Ops:
  0.6 30.7 %exchange.1 = (f32[1,1024]{1,0:T(1,128)}, f32[2,128]{1,0:T(2,128)}, f32[16,8,128]{2,1,0:T(8,128)}, f32[1,128]{1,0:T(1,128)}, f32[9,3,4,512]{3,2,1,0:T(4,128)}, /*index=5*/f32[2,32,128]{2,1,0:T(8,128)}) custom-call(s32[2]{0:T(128)} %count_ref.1, s32[2,26]{1,0:T(2,128)} %near_ref.1, f32[3,1024]{1,0:T(4,128)} %pos_ref.1, f32[1,1024]{1,0:T(1,128)} %bitcast.3, ...), custom_call_target="tpu_custom_call" | custom-call | tf_op jit(solution)/shard_map/exchange/pallas_call | solution.py:426
  31.3 6.6 %top.1 = (f32[1,1024]{1,0:T(1,128)}, f32[2,128]{1,0:T(2,128)}, f32[1,8,128]{2,1,0:T(8,128)}, f32[1,8]{1,0:T(1,128)}) custom-call(f32[1,1024]{1,0:T(1,128)} %get-tuple-element.14.near_ref, f32[2,128]{1,0:T(2,128)} %get-tuple-element.15.coeffs_ref, f32[16,8,128]{2,1,0:T(8,128)} %get-tuple-element.16.gram_ref, f32[1,128]{1,0:T(1,128)} %get-tuple-element.17.moment_ref, ...), custom_call_target="tpu_custom_call" | custom-call | tf_op jit(solution)/shard_map/top/pallas_call | solution.py:465

commit v4 on v3

--- a/solution.py
+++ b/solution.py
@@ -117,14 +117,23 @@
     count, rank = work.shape[0], work.shape[1]
     row = lax.broadcasted_iota(jnp.int32, (count, PANEL, rank), 1)
     col = lax.broadcasted_iota(jnp.int32, (count, PANEL, rank), 2)
+
+    def spread(rows, low):
+        return [
+            jnp.broadcast_to(rows[:, :, low + j : low + j + 1], (count, PANEL, rank))
+            for j in range(PANEL)
+        ]
+
+    low = panels[0] * PANEL
+    panel = work[:, low : low + PANEL, 0:rank]
+    right = work[:, low : low + PANEL, rank:]
     for low in (p * PANEL for p in panels):
         high = low + PANEL
-        panel = work[:, low:high, 0:rank]
-        right = work[:, low:high, rank:]
-        columns = [
-            jnp.broadcast_to(panel[:, :, low + j : low + j + 1], (count, PANEL, rank))
-            for j in range(PANEL)
-        ]
+        columns = spread(panel, low)
+        if high < rank:
+            after = work[:, high : high + PANEL, 0:rank]
+            after_right = work[:, high : high + PANEL, rank:]
+            after_columns = spread(after, low)
         done = jnp.zeros((count, PANEL, rank), jnp.float32)
         done_right = done
         for j in range(PANEL):
@@ -137,15 +146,25 @@
             pivot_right = right[:, j : j + 1] * inverse
             done = jnp.where(row == j, pivot, done)
             done_right = jnp.where(row == j, pivot_right, done_right)
+            scaled = [columns[k][:, j : j + 1, :] * inverse for k in range(j + 1, PANEL)]
             if j + 1 < PANEL:
                 panel = panel - below * pivot
                 right = right - below * pivot_right
                 for k in range(j + 1, PANEL):
-                    columns[k] = columns[k] - below * (columns[k][:, j : j + 1, :] * inverse)
+                    columns[k] = columns[k] - below * scaled[k - j - 1]
+            if high < rank:
+                further = after_columns[j] * inverse
+                after = after - further * pivot
+                after_right = after_right - further * pivot_right
+                for k in range(j + 1, PANEL):
+                    after_columns[k] = after_columns[k] - further * scaled[k - j - 1]
         done = jnp.where(col >= row + low, done, 0.0)
         upper[:, low:high, 0:rank] = done
         upper[:, low:high, rank:] = done_right
         if high < rank:
+            panel, right = after, after_right
+        rest = high + PANEL
+        if rest < rank:
             for i in range(count):
                 a, b, c = split3(jnp.concatenate([done[i], done_right[i]], 1))
                 left = jnp.concatenate([a, b, c, a, b, a], 0)[:, 0:rank]
@@ -153,7 +172,10 @@
                 update = jnp.dot(
                     left.T.astype(jnp.bfloat16), both, preferred_element_type=jnp.float32
                 )
-                work[i, high:, :] = work[i, high:, :] - update[high:]
+                work[i, rest:, :] = work[i, rest:, :] - update[rest:]
+    if high < rank:
+        work[:, high : high + PANEL, 0:rank] = panel
+        work[:, high : high + PANEL, rank:] = right
 
 
 def diagonal_row(columns):
@@ -348,8 +370,7 @@
         for slot in late:
             forwards[slot].wait_recv()
         sources = [(slot, 2) for slot in late]
-        if group != GROUPS[-1]:
-            sources += [(slot, w) for slot in group for w in range(2)]
+        sources += [(slot, w) for slot in group for w in range(2)]
         work_left = near(sources)
         if group == GROUPS[0]:
             tiles = len(late) + 4 * len(group)
@@ -359,10 +380,12 @@
         for _ in work_left:
             pass
         late = group
+    for slot in late:
+        forwards[slot].wait_recv()
+    for _ in near([(slot, 2) for slot in late]):
+        pass
     for t in range(2):
         near_out[:, t * size : (t + 1) * size] = lane_sums(totals[t])
-    for slot in late:
-        forwards[slot].wait_recv()
     for copy in rs + list(window.values()) + list(forwards.values()):
         copy.wait_send()
     for copy in ag:
@@ -374,37 +397,20 @@
     coeffs_ref,
     gram_ref,
     moment_ref,
-    win_ref,
-    weights,
     near_out,
     coeffs_out,
     factor_out,
     top_coeffs_out,
-    targets,
-    totals,
     work,
     upper,
 ):
-    block = lax.axis_index("leaf")
     node = lax.axis_index("node")
-    half = place(node)[2]
-    centre = centre_of(block, node)
     rank = work.shape[1]
-    size = win_ref.shape[3]
-    for t in range(2):
-        targets[t] = target_features(centred(win_ref[4, t, 0:3, :], centre))
-    totals[...] = jnp.zeros_like(totals)
-    sources = [(slot, w) for slot in GROUPS[-1] for w in range(3)]
-    near = near_work(sources, half, centre, win_ref, weights, targets, totals)
-    pieces = 5 * len(GROUPS[-1]) * (size // PIECE)
-
+    near_out[...] = near_ref[...]
     coeffs_out[...] = coeffs_ref[...]
     work[0, :, 0:rank] = gram_ref[...].reshape(rank, rank)
     work[0, :, rank:] = jnp.broadcast_to(moment_ref[...], (rank, rank)).T
-    factorize(work, upper, range(rank // PANEL), near, pieces)
-    for t in range(2):
-        lanes = slice(t * size, (t + 1) * size)
-        near_out[:, lanes] = near_ref[:, lanes] + lane_sums(totals[t])
+    factorize(work, upper, range(rank // PANEL))
     work[0, :, 0:rank] = upper[0, :, 0:rank].T
     rows = factor_out.shape[1]
     mine = pl.ds(pl.multiple_of(node * rows, rows), rows)
@@ -423,19 +429,19 @@
     shape = lambda *dims: jax.ShapeDtypeStruct(dims, jnp.float32)
     scratch = lambda *dims: pltpu.VMEM(dims, jnp.float32)
     semaphores = lambda n: pltpu.SemaphoreType.DMA((n,))
-    near, coeffs, top_gram, top_moment, window, weights = pl.pallas_call(
+    near, coeffs, top_gram, top_moment = pl.pallas_call(
         functools.partial(exchange_kernel, blocks, nodes),
         out_shape=(
             shape(1, 2 * size),
             shape(2, rank),
             shape(nodes, rows, rank),
             shape(1, rank),
-            shape(9, 3, 4, size),
-            shape(2, 32, 128),
         ),
         in_specs=[smem] + [vmem] * 3 + [pl.BlockSpec(memory_space=pl.ANY)] + [vmem] * 2,
-        out_specs=(vmem,) * 6,
+        out_specs=(vmem,) * 4,
         scratch_shapes=[
+            scratch(9, 3, 4, size),
+            scratch(2, 32, 128),
             scratch(2 * size, rank),
             pltpu.VMEM((2, size, 64), jnp.bfloat16),
             scratch(2, size, 128),
@@ -465,16 +471,14 @@
     near, coeffs, factor, top_coeffs = pl.pallas_call(
         top_kernel,
         out_shape=(shape(1, 2 * size), shape(2, rank), shape(1, rows, rank), shape(1, rows)),
-        in_specs=[vmem] * 6,
+        in_specs=[vmem] * 4,
         out_specs=(vmem,) * 4,
         scratch_shapes=[
-            pltpu.VMEM((2, size, 64), jnp.bfloat16),
-            scratch(2, size, 128),
             scratch(1, rank, 2 * rank),
             scratch(1, rank, 2 * rank),
         ],
         name="top",
-    )(near, coeffs, top_gram, top_moment, window, weights)
+    )(near, coeffs, top_gram, top_moment)
     return (near.reshape(-1), coeffs, factor, top_coeffs)
 
 

time: 38.2 us -> 37.6 us (0.984)
  Pallas kernels: 37.3 us -> 36.7 us
    pallas_call x1, Pallas kernels: 6.62 us -> 4.26 us  [body(): pl.pallas_call(top_kernel, out_shape=(shape(1, 2 * size), shape(2, rank),...]
    pallas_call x1, Pallas kernels: 30.7 us -> 32.5 us  [body(): pl.pallas_call(functools.partial(exchange_kernel, blocks, nodes), out_sha...]
where the time goes in v4:
time: 37.6 us; the launch traced here: 37.4 us
  Pallas kernels  36.7 us (98%)
  between operations  0.64 us (2%)
    pallas_call x1, Pallas kernels, body(): pl.pallas_call(functools.partial(exchange_kernel, blocks, nodes), out_sha...  32.5 us
    pallas_call x1, Pallas kernels, body(): pl.pallas_call(top_kernel, out_shape=(shape(1, 2 * size), shape(2, rank),...  4.26 us

profile of v4, /device:TPU:1, one launch (start us, length us, event | category | flops | bytes accessed | tf_op | source)
XLA Modules:
  0.0 37.4 jit_solution(9864772761067734369)
XLA Ops:
  0.6 32.5 %exchange.1 = (f32[1,1024]{1,0:T(1,128)}, f32[2,128]{1,0:T(2,128)}, f32[16,8,128]{2,1,0:T(8,128)}, f32[1,128]{1,0:T(1,128)}) custom-call(s32[2]{0:T(128)} %count_ref.1, s32[2,26]{1,0:T(2,128)} %near_ref.1, f32[3,1024]{1,0:T(4,128)} %pos_ref.1, f32[1,1024]{1,0:T(1,128)} %bitcast.3, f32[1024,128]{1,0:T(8,128)} %far_hbm.1, f32[3,2,128]{2,1,0:T(2,128)} %bitcast.4, ...), custom_call_target="tpu_custom_call" | custom-call | tf_op jit(solution)/shard_map/exchange/pallas_call | solution.py:432
  33.1 4.3 %top.1 = (f32[1,1024]{1,0:T(1,128)}, f32[2,128]{1,0:T(2,128)}, f32[1,8,128]{2,1,0:T(8,128)}, f32[1,8]{1,0:T(1,128)}) custom-call(f32[1,1024]{1,0:T(1,128)} %get-tuple-element.12.near_ref, f32[2,128]{1,0:T(2,128)} %get-tuple-element.13.coeffs_ref, f32[16,8,128]{2,1,0:T(8,128)} %get-tuple-element.14.gram_ref, f32[1,128]{1,0:T(1,128)} %get-tuple-element.15.moment_ref), custom_call_target="tpu_custom_call" | custom-call | tf_op jit(solution)/shard_map/top/pallas_call | solution.py:471

commit v5 on v4

--- a/solution.py
+++ b/solution.py
@@ -13,7 +13,8 @@
 PIECE = 128
 MESH = pl.DeviceIdType.MESH
 HIGHEST = lax.Precision.HIGHEST
-EARLY = 6
+LATE = ((8, 0), (8, 1), (8, 2))
+EARLY = 7
 GROUPS = ((3, 5), (0, 1, 2), (6, 7, 8))
 
 
@@ -75,7 +76,7 @@
         leaf = base + lax.rem(y + dy + ACROSS, ACROSS) * ACROSS + z
         ids = jnp.where(row == k, leaf, ids)
     for t in range(2):
-        hit = (near_ref[t : t + 1, :] == ids) & (lane < count_ref[t])
+        hit = (near_ref[t : t + 1, :] == ids) & (lane < count_ref[0:1, t : t + 1])
         weight = jnp.sum(jnp.where(hit, 1.0, 0.0), 1, keepdims=True)
         own = row[:, 0:1] == 12 + t
         weights[t] = jnp.broadcast_to(jnp.where(own, 1.0, weight), (32, 128))
@@ -187,27 +188,34 @@
 def exchange_kernel(
     blocks,
     nodes,
-    count_ref,
-    near_ref,
-    pos_ref,
-    charge_ref,
+    count_hbm,
+    near_hbm,
+    pos_hbm,
+    charge_hbm,
     far_hbm,
-    proxy_ref,
-    strength_ref,
+    proxy_hbm,
+    strength_hbm,
     near_out,
     coeffs_out,
     top_gram_ref,
     top_moment_ref,
     win_ref,
     weights,
+    targets,
     far_ref,
-    targets,
+    count_ref,
+    near_ref,
+    pos_ref,
+    charge_ref,
+    proxy_ref,
+    strength_ref,
     totals,
     work,
     upper,
     share,
     parts,
     far_sem,
+    input_sem,
     win_send,
     win_recv,
     rs_send,
@@ -231,14 +239,6 @@
     def in_block(k):
         return (block, lax.rem(node + k, nodes))
 
-    far_copies = []
-    for t in range(2):
-        lanes = pl.ds(t * size, size)
-        far_copies.append(
-            pltpu.make_async_copy(far_hbm.at[lanes], far_ref.at[lanes], far_sem.at[t])
-        )
-        far_copies[t].start()
-
     outside = 1 - 2 * slab
     barrier = pltpu.get_barrier_semaphore()
     for k in range(1, nodes):
@@ -248,6 +248,31 @@
             target = spatial(-outside, dy, core)
             pl.semaphore_signal(barrier, inc=1, device_id=target, device_id_type=MESH)
 
+    copies = [
+        pltpu.make_async_copy(source, target, input_sem.at[i])
+        for i, (source, target) in enumerate(
+            (
+                (pos_hbm, pos_ref),
+                (charge_hbm, charge_ref),
+                (proxy_hbm, proxy_ref),
+                (strength_hbm, strength_ref),
+                (near_hbm, near_ref),
+                (count_hbm, count_ref),
+            )
+        )
+    ]
+    for copy in copies:
+        copy.start()
+    far_copies = []
+    for t in range(2):
+        lanes = pl.ds(t * size, size)
+        far_copies.append(
+            pltpu.make_async_copy(far_hbm.at[lanes], far_ref.at[lanes], far_sem.at[t])
+        )
+        far_copies[t].start()
+
+    for copy in copies:
+        copy.wait()
     for t in range(2):
         lanes = slice(t * size, (t + 1) * size)
         win_ref[4, t, 0:3, :] = pos_ref[:, lanes]
@@ -371,6 +396,7 @@
             forwards[slot].wait_recv()
         sources = [(slot, 2) for slot in late]
         sources += [(slot, w) for slot in group for w in range(2)]
+        sources = [source for source in sources if source not in LATE]
         work_left = near(sources)
         if group == GROUPS[0]:
             tiles = len(late) + 4 * len(group)
@@ -382,7 +408,7 @@
         late = group
     for slot in late:
         forwards[slot].wait_recv()
-    for _ in near([(slot, 2) for slot in late]):
+    for _ in near([(slot, 2) for slot in late if (slot, 2) not in LATE]):
         pass
     for t in range(2):
         near_out[:, t * size : (t + 1) * size] = lane_sums(totals[t])
@@ -397,20 +423,32 @@
     coeffs_ref,
     gram_ref,
     moment_ref,
+    win_ref,
+    weights,
+    targets,
     near_out,
     coeffs_out,
     factor_out,
     top_coeffs_out,
+    totals,
     work,
     upper,
 ):
+    block = lax.axis_index("leaf")
     node = lax.axis_index("node")
+    half = place(node)[2]
     rank = work.shape[1]
-    near_out[...] = near_ref[...]
+    size = win_ref.shape[3]
+    totals[...] = jnp.zeros_like(totals)
+    near = near_work(LATE, half, centre_of(block, node), win_ref, weights, targets, totals)
+    pieces = sum(2 if w < 2 else 1 for _, w in LATE) * (size // PIECE)
     coeffs_out[...] = coeffs_ref[...]
     work[0, :, 0:rank] = gram_ref[...].reshape(rank, rank)
     work[0, :, rank:] = jnp.broadcast_to(moment_ref[...], (rank, rank)).T
-    factorize(work, upper, range(rank // PANEL))
+    factorize(work, upper, range(rank // PANEL), near, pieces)
+    for t in range(2):
+        lanes = slice(t * size, (t + 1) * size)
+        near_out[:, lanes] = near_ref[:, lanes] + lane_sums(totals[t])
     work[0, :, 0:rank] = upper[0, :, 0:rank].T
     rows = factor_out.shape[1]
     mine = pl.ds(pl.multiple_of(node * rows, rows), rows)
@@ -425,31 +463,37 @@
     rank = far_sample.shape[1]
     rows = rank // nodes
     vmem = pl.BlockSpec(memory_space=pltpu.VMEM)
-    smem = pl.BlockSpec(memory_space=pltpu.SMEM)
     shape = lambda *dims: jax.ShapeDtypeStruct(dims, jnp.float32)
     scratch = lambda *dims: pltpu.VMEM(dims, jnp.float32)
     semaphores = lambda n: pltpu.SemaphoreType.DMA((n,))
-    near, coeffs, top_gram, top_moment = pl.pallas_call(
+    parts = pl.pallas_call(
         functools.partial(exchange_kernel, blocks, nodes),
         out_shape=(
-            shape(1, 2 * size),
-            shape(2, rank),
-            shape(nodes, rows, rank),
-            shape(1, rank),
-        ),
-        in_specs=[smem] + [vmem] * 3 + [pl.BlockSpec(memory_space=pl.ANY)] + [vmem] * 2,
-        out_specs=(vmem,) * 4,
-        scratch_shapes=[
+            scratch(1, 2 * size),
+            scratch(2, rank),
+            scratch(nodes, rows, rank),
+            scratch(1, rank),
             scratch(9, 3, 4, size),
             scratch(2, 32, 128),
+            pltpu.VMEM((2, size, 64), jnp.bfloat16),
+        ),
+        in_specs=[pl.BlockSpec(memory_space=pl.ANY)] * 7,
+        out_specs=(vmem,) * 7,
+        scratch_shapes=[
             scratch(2 * size, rank),
-            pltpu.VMEM((2, size, 64), jnp.bfloat16),
+            pltpu.VMEM((1, 2), jnp.int32),
+            pltpu.VMEM(near_list.shape, jnp.int32),
+            scratch(3, 2 * size),
+            scratch(1, 2 * size),
+            scratch(3, 2, rank),
+            scratch(2, rank),
             scratch(2, size, 128),
             scratch(2, rank, 2 * rank),
             scratch(2, rank, 2 * rank),
             scratch(nodes, rows + 1, rank),
             scratch(nodes, rows + 1, rank),
             semaphores(2),
+            semaphores(6),
             semaphores(18),
             semaphores(18),
             semaphores(nodes),
@@ -460,7 +504,7 @@
         compiler_params=pltpu.CompilerParams(collective_id=0, has_side_effects=True),
         name="exchange",
     )(
-        near_count,
+        near_count[None, :],
         near_list,
         positions,
         charges[None, :],
@@ -471,14 +515,15 @@
     near, coeffs, factor, top_coeffs = pl.pallas_call(
         top_kernel,
         out_shape=(shape(1, 2 * size), shape(2, rank), shape(1, rows, rank), shape(1, rows)),
-        in_specs=[vmem] * 4,
+        in_specs=[vmem] * 7,
         out_specs=(vmem,) * 4,
         scratch_shapes=[
+            scratch(2, size, 128),
             scratch(1, rank, 2 * rank),
             scratch(1, rank, 2 * rank),
         ],
         name="top",
-    )(near, coeffs, top_gram, top_moment)
+    )(*(pltpu.with_memory_space_constraint(part, pltpu.VMEM) for part in parts))
     return (near.reshape(-1), coeffs, factor, top_coeffs)
 
 

time: 37.6 us -> 34.6 us (0.920)
  Pallas kernels: 36.7 us -> 33.8 us
    pallas_call x1, Pallas kernels: 32.5 us -> 29.8 us  [body(): pl.pallas_call(functools.partial(exchange_kernel, blocks, nodes), out_sha...]
where the time goes in v5:
time: 34.6 us; the launch traced here: 34.5 us
  Pallas kernels  33.8 us (98%)
  between operations  0.64 us (2%)
    pallas_call x1, Pallas kernels, body(): pl.pallas_call(functools.partial(exchange_kernel, blocks, nodes), out_sha...  29.8 us
    pallas_call x1, Pallas kernels, body(): pl.pallas_call(top_kernel, out_shape=(shape(1, 2 * size), shape(2, rank),...  3.98 us

profile of v5, /device:TPU:1, one launch (start us, length us, event | category | flops | bytes accessed | tf_op | source)
XLA Modules:
  0.0 34.5 jit_solution(2241547513500688272)
XLA Ops:
  0.6 29.8 %exchange.1 = (f32[1,1024]{1,0:T(1,128)S(1)}, f32[2,128]{1,0:T(2,128)S(1)}, f32[16,8,128]{2,1,0:T(8,128)S(1)}, f32[1,128]{1,0:T(1,128)S(1)}, f32[9,3,4,512]{3,2,...) custom-call(s32[1,2]{1,0:T(1,128)} %bitcast.6, s32[2,26]{1,0:T(2,128)} %near_hbm.1, ...), custom_call_target="tpu_custom_call" | custom-call | tf_op jit(solution)/shard_map/exchange/pallas_call | solution.py:469
  30.5 4.0 %top.1 = (f32[1,1024]{1,0:T(1,128)}, f32[2,128]{1,0:T(2,128)}, f32[1,8,128]{2,1,0:T(8,128)}, f32[1,8]{1,0:T(1,128)}) custom-call(f32[1,1024]{1,0:T(1,128)S(1)} %get-tuple-element.15.near_ref, f32[2,128]{1,0:T(2,128)S(1)} %get-tuple-element.16.coeffs_ref, f32[16,8,128]{2,1,0:T(8,128)S(1)} %get-tuple-element.17.gram_ref, ...), custom_call_target="tpu_custom_call" | custom-call | tf_op jit(solution)/shard_map/top/pallas_call | solution.py:515

commit v6 on v5

--- a/solution.py
+++ b/solution.py
@@ -240,8 +240,9 @@
         return (block, lax.rem(node + k, nodes))
 
     outside = 1 - 2 * slab
+    farthest = sorted(range(1, nodes), key=lambda k: -min(k, nodes - k))
     barrier = pltpu.get_barrier_semaphore()
-    for k in range(1, nodes):
+    for k in farthest:
         pl.semaphore_signal(barrier, inc=1, device_id=in_block(k), device_id_type=MESH)
     for dy in (-1, 0, 1):
         for core in (0, 1):
@@ -313,7 +314,7 @@
     pl.semaphore_wait(barrier, nodes - 1 + 6)
 
     rs = []
-    for k in range(1, nodes):
+    for k in farthest:
         target = in_block(k)
         rs.append(
             pltpu.make_async_remote_copy(
@@ -374,7 +375,7 @@
     top_gram_ref[node] = sums[0:rows]
     top_moment_ref[...] = sums[rows : rows + 1]
     ag = []
-    for k in range(1, nodes):
+    for k in farthest:
         ag.append(
             pltpu.make_async_remote_copy(
                 src_ref=top_gram_ref.at[node],

time: 34.6 us -> 34.5 us (level)
  no operation moved by 1% of the time
where the time goes in v6:
time: 34.5 us; the launch traced here: 34.3 us
  Pallas kernels  33.7 us (98%)
  between operations  0.64 us (2%)
    pallas_call x1, Pallas kernels, body(): pl.pallas_call(functools.partial(exchange_kernel, blocks, nodes), out_sha...  29.7 us
    pallas_call x1, Pallas kernels, body(): pl.pallas_call(top_kernel, out_shape=(shape(1, 2 * size), shape(2, rank),...  3.98 us

profile of v6, /device:TPU:1, one launch (start us, length us, event | category | flops | bytes accessed | tf_op | source)
XLA Modules:
  0.0 34.3 jit_solution(6149551435266861863)
XLA Ops:
  0.6 29.7 %exchange.1 = (f32[1,1024]{1,0:T(1,128)S(1)}, f32[2,128]{1,0:T(2,128)S(1)}, f32[16,8,128]{2,1,0:T(8,128)S(1)}, f32[1,128]{1,0:T(1,128)S(1)}, f32[9,3,4,512]{3,2,...) custom-call(s32[1,2]{1,0:T(1,128)} %bitcast.6, s32[2,26]{1,0:T(2,128)} %near_hbm.1, ...), custom_call_target="tpu_custom_call" | custom-call | tf_op jit(solution)/shard_map/exchange/pallas_call | solution.py:470
  30.4 4.0 %top.1 = (f32[1,1024]{1,0:T(1,128)}, f32[2,128]{1,0:T(2,128)}, f32[1,8,128]{2,1,0:T(8,128)}, f32[1,8]{1,0:T(1,128)}) custom-call(f32[1,1024]{1,0:T(1,128)S(1)} %get-tuple-element.15.near_ref, f32[2,128]{1,0:T(2,128)S(1)} %get-tuple-element.16.coeffs_ref, f32[16,8,128]{2,1,0:T(8,128)S(1)} %get-tuple-element.17.gram_ref, ...), custom_call_target="tpu_custom_call" | custom-call | tf_op jit(solution)/shard_map/top/pallas_call | solution.py:516
